TPU v7x, 32 devices: a whole 2x2x4 slice. The times are simulated.
32 devices in a mesh: parts: 2 (over x), outer: 8 (over z, y), inner: 2 (over core).
Axes of the slice: x: 2, y: 2, z: 4, core: 2. Of those that a mesh axis runs over, the one named last changes fastest.
Arguments:
- state: float32 [2, 8388608], P(None, ('parts', 'outer', 'inner')), parts along dimension 1, may hold values from -6 to 6
- gates: bfloat16 [8, 2, 128, 128], replicated, may hold values from -0.375 to 0.375
- bonds: float32 [8, 2, 2, 128], replicated, may hold values from -4 to 4
- order: int32 [8], replicated, may hold values from 0 to 7, each once
- slice_bits: int32 [16], P('parts'), parts along dimension 0, may hold values from 0 to 1
Outputs:
- result: float32 [2, 8388608], P(None, ('parts', 'outer', 'inner')), parts along dimension 1
There are 2 independent parts, one for each index of `parts`. A program takes and returns all parts, laid end to end along the dimension named above; an argument that names none is the same for every part. Nothing has to cross between parts.
Inputs may be any that keep to these rules, and one draw needn't show every extreme that they name: `order`: each branch matrix is named once.
All inputs are finite; a program needn't handle non-finite values.
Results may differ from a plain program's by a relative error of at most 0.0003.
Values sent between devices are 32-bit elements; how exact they have to be, the bound alone decides.
No kernel may reach another device: no remote copies, remote signals or barrier semaphores. Data moves between devices by JAX's collectives and lax.ppermute only.
A program may use at most 64 MiB of HBM per device.

v0:
```python
import functools

import jax
import jax.numpy as jnp
from jax import lax
from jax.experimental import pallas as pl
from jax.experimental.pallas import tpu as pltpu
from jax.sharding import PartitionSpec as P

UNROLL = 8


def build_weights(gate_ref, weight_ref):
    dim = gate_ref.shape[-1]
    real = gate_ref[0, 0].astype(jnp.float32).T.astype(jnp.bfloat16)
    imag = gate_ref[0, 1].astype(jnp.float32).T.astype(jnp.bfloat16)
    weight_ref[:dim, :dim] = real
    weight_ref[:dim, dim:] = imag
    weight_ref[dim:, :dim] = -imag
    weight_ref[dim:, dim:] = real


def contract(load, store, weight_ref, bond_ref, groups):
    bond_real = bond_ref[0, 0, 0:1, :]
    bond_imag = bond_ref[0, 0, 1:2, :]
    unroll = min(UNROLL, groups)

    def some(index, carry):
        high, low = [], []
        for k in range(unroll):
            real, imag = load(index * unroll + k)
            real, imag = real.T, imag.T
            scaled = jnp.concatenate(
                [real * bond_real - imag * bond_imag, real * bond_imag + imag * bond_real], axis=1
            )
            head = scaled.astype(jnp.bfloat16)
            high.append(head)
            low.append((scaled - head.astype(jnp.float32)).astype(jnp.bfloat16))
        product = jnp.dot(
            jnp.concatenate(high + low, axis=0), weight_ref[...], preferred_element_type=jnp.float32
        )
        half = product.shape[0] // 2
        product = product[:half] + product[half:]
        size = half // unroll
        for k in range(unroll):
            store(index * unroll + k, product[k * size : (k + 1) * size])
        return carry

    lax.fori_loop(0, groups // unroll, some, 0)


def kernel(order_ref, bits_ref, *refs, steps, n_in, n_out, in_axis, out_axis, rows):
    del order_ref, bits_ref
    refs = list(refs)
    ins = [refs.pop(0) for _ in range(n_in)]
    gates = [refs.pop(0) for _ in range(steps)]
    bonds = [refs.pop(0) for _ in range(steps)]
    outs = [refs.pop(0) for _ in range(n_out)]
    weight_ref, bufs, in_sem, out_sem = refs
    dim = weight_ref.shape[-1] // 2
    groups = rows // dim

    if in_axis is not None:
        me = lax.axis_index(in_axis)
        part = rows // n_in
        copies = []
        for k in range(n_in):
            start = pl.multiple_of(lax.rem(me + (n_in - k), n_in) * part, part)
            for c in range(2):
                copies.append(
                    pltpu.make_async_copy(
                        ins[k].at[c], bufs.at[0, c, pl.ds(start, part), :], in_sem.at[k, c]
                    )
                )
                copies[-1].start()

    for s in range(steps):
        build_weights(gates[s], weight_ref.at[s])
    if in_axis is not None:
        for copy in copies:
            copy.wait()

    def load_interleaved(g):
        return tuple(ins[0][pl.ds(2 * g + c, dim, stride=2 * groups), :] for c in range(2))

    def loader(which):
        def load(g):
            return tuple(bufs[which, c, pl.ds(g, dim, stride=groups), :] for c in range(2))

        return load

    def storer(which):
        def store(g, value):
            for c in range(2):
                bufs[which, c, pl.ds(pl.multiple_of(g * dim, dim), dim), :] = value[
                    :, c * dim : (c + 1) * dim
                ]

        return store

    def store_interleaved(g, value):
        for c in range(2):
            outs[0][pl.ds(2 * g * dim + c, dim, stride=2), :] = value[:, c * dim : (c + 1) * dim]

    for s in range(steps):
        load = load_interleaved if in_axis is None and s == 0 else loader(s % 2)
        last = out_axis is None and s == steps - 1
        store = store_interleaved if last else storer((s + 1) % 2)
        contract(load, store, weight_ref.at[s], bonds[s], groups)

    if out_axis is not None:
        me = lax.axis_index(out_axis)
        part = rows // n_out
        copies = []
        for k in range(n_out):
            start = pl.multiple_of(lax.rem(me + k, n_out) * part, part)
            for c in range(2):
                copies.append(
                    pltpu.make_async_copy(
                        bufs.at[steps % 2, c, pl.ds(start, part), :], outs[k].at[c], out_sem.at[k, c]
                    )
                )
                copies[-1].start()
        for copy in copies:
            copy.wait()


def call(ins, gates, bonds, order, bits, first, steps, rows, n_out, in_axis, out_axis):
    dim = gates.shape[-1]
    n_in = len(ins)

    def gate_map(k, i, order, bits):
        return (order[first + k], 0, 0, 0)

    def bond_map(k, i, order, bits):
        return (order[first + k], bits[first + k], 0, 0)

    anywhere = pl.BlockSpec(memory_space=pl.ANY)
    flat = pl.BlockSpec((2 * rows, dim), lambda i, order, bits: (0, 0))
    in_specs = [flat] if in_axis is None else [anywhere] * n_in
    in_specs += [
        pl.BlockSpec((1,) + gates.shape[1:], functools.partial(gate_map, k)) for k in range(steps)
    ]
    in_specs += [
        pl.BlockSpec((1, 1) + bonds.shape[2:], functools.partial(bond_map, k)) for k in range(steps)
    ]
    if out_axis is None:
        out_shape = [jax.ShapeDtypeStruct((2 * rows, dim), jnp.float32)]
        out_specs = [flat]
    else:
        out_shape = [jax.ShapeDtypeStruct((2, rows // n_out, dim), jnp.float32)] * n_out
        out_specs = [anywhere] * n_out
    return pl.pallas_call(
        functools.partial(
            kernel,
            steps=steps,
            n_in=n_in,
            n_out=n_out,
            in_axis=in_axis,
            out_axis=out_axis,
            rows=rows,
        ),
        out_shape=out_shape,
        grid_spec=pltpu.PrefetchScalarGridSpec(
            num_scalar_prefetch=2,
            grid=(1,),
            in_specs=in_specs,
            out_specs=out_specs,
            scratch_shapes=[
                pltpu.VMEM((steps, 2 * dim, 2 * dim), jnp.bfloat16),
                pltpu.VMEM((2, 2, rows, dim), jnp.float32),
                pltpu.SemaphoreType.DMA((n_in, 2)),
                pltpu.SemaphoreType.DMA((n_out, 2)),
            ],
        ),
        cost_estimate=pl.CostEstimate(
            flops=steps * 16 * rows * dim * dim, bytes_accessed=16 * rows * dim, transcendentals=0
        ),
    )(order, bits, *ins, *([gates] * steps), *([bonds] * steps))


def exchange(pieces, axis):
    n = len(pieces)
    return [pieces[0]] + [
        lax.ppermute(pieces[k], axis, [(i, (i + k) % n) for i in range(n)]) for k in range(1, n)
    ]


def body(state, gates, bonds, order, bits):
    dim = gates.shape[-1]
    rows = state.shape[1] // dim
    leading = lax.axis_size("outer")
    second = lax.axis_size("inner")
    flat = state.reshape(2, rows, dim).transpose(1, 0, 2).reshape(2 * rows, dim)
    run = functools.partial(call, gates=gates, bonds=bonds, order=order, bits=bits, rows=rows)
    pieces = run([flat], first=0, steps=3, n_out=leading, in_axis=None, out_axis="outer")
    pieces = exchange(pieces, "outer")
    pieces = run(pieces, first=3, steps=3, n_out=second, in_axis="outer", out_axis="inner")
    pieces = exchange(pieces, "inner")
    (flat,) = run(pieces, first=6, steps=2, n_out=1, in_axis="inner", out_axis=None)
    return flat.reshape(rows, 2, dim).transpose(1, 0, 2).reshape(2, rows * dim)


def solution(mesh):
    in_specs = (P(None, ("parts", "outer", "inner")), P(), P(), P(), P("parts"))
    out_specs = P(None, ("parts", "outer", "inner"))
    return jax.shard_map(body, mesh=mesh, in_specs=in_specs, out_specs=out_specs, check_vma=False)
```

profile of v0, /device:TPU:13, one launch (start us, length us, event | category | flops | bytes accessed | tf_op | source)
XLA Modules:
  0.0 79.8 jit_solution(10594444149582811333)
XLA Ops:
  0.0 8.7 %shard_map.55 = (f32[2,256,128]{2,1,0:T(8,128)}, f32[2,256,128]{2,1,0:T(8,128)}, f32[2,256,128]{2,1,0:T(8,128)}, f32[2,256,128]{2,1,0:T(8,128)}, f32[2,256,128]{...) custom-call(s32[8]{0:T(128)} %order_ref.5, s32[8]{0:T(128)} %bits_ref.5, ...), custom_call_target="tpu_custom_call" | custom-call | flops 1610612736 | bytes 4194304 | tf_op jit(solution)/shard_map/pallas_call | solution.py:153
  8.7 1.3 %collective-permute-start = (f32[2,256,128]{2,1,0:T(8,128)}, f32[2,256,128]{2,1,0:T(8,128)S(1)}, u32[]{:S(2)}, u32[]{:S(2)}) collective-permute-start(f32[2,256,128]{2,1,0:T(8,128)} %get-tuple-element.16), channel_id=1, source_target_pairs={{0,2},{2,4},{4,6},{6,8},{8,10},{10,12},{12,14},{14,0},{1,3},{3,5},... | collective-permute-start | bytes 786440 | tf_op jit(solution)/shard_map/ppermute | solution.py:185
  10.0 1.3 %collective-permute-start.1 = (f32[2,256,128]{2,1,0:T(8,128)}, f32[2,256,128]{2,1,0:T(8,128)S(1)}, u32[]{:S(2)}, u32[]{:S(2)}) collective-permute-start(f32[2,256,128]{2,1,0:T(8,128)} %get-tuple-element.17), channel_id=1, source_target_pairs={{0,4},{2,6},{4,8},{6,10},{8,12},{10,14},{12,0},{14,2},{1,5},{3,7},... | collective-permute-start | bytes 786440 | tf_op jit(solution)/shard_map/ppermute | solution.py:185
  11.2 1.0 %collective-permute-start.2 = (f32[2,256,128]{2,1,0:T(8,128)}, f32[2,256,128]{2,1,0:T(8,128)S(1)}, u32[]{:S(2)}, u32[]{:S(2)}) collective-permute-start(f32[2,256,128]{2,1,0:T(8,128)} %get-tuple-element.18), channel_id=1, source_target_pairs={{0,6},{2,8},{4,10},{6,12},{8,14},{10,0},{12,2},{14,4},{1,7},{3,9},... | collective-permute-start | bytes 786440 | tf_op jit(solution)/shard_map/ppermute | solution.py:185
  12.2 1.3 %collective-permute-start.3 = (f32[2,256,128]{2,1,0:T(8,128)}, f32[2,256,128]{2,1,0:T(8,128)S(1)}, u32[]{:S(2)}, u32[]{:S(2)}) collective-permute-start(f32[2,256,128]{2,1,0:T(8,128)} %get-tuple-element.19), channel_id=1, source_target_pairs={{0,8},{2,10},{4,12},{6,14},{8,0},{10,2},{12,4},{14,6},{1,9},{3,11}... | collective-permute-start | bytes 786440 | tf_op jit(solution)/shard_map/ppermute | solution.py:185
  13.6 1.0 %collective-permute-start.4 = (f32[2,256,128]{2,1,0:T(8,128)}, f32[2,256,128]{2,1,0:T(8,128)S(1)}, u32[]{:S(2)}, u32[]{:S(2)}) collective-permute-start(f32[2,256,128]{2,1,0:T(8,128)} %get-tuple-element.20), channel_id=1, source_target_pairs={{0,10},{2,12},{4,14},{6,0},{8,2},{10,4},{12,6},{14,8},{1,11},{3,13... | collective-permute-start | bytes 786440 | tf_op jit(solution)/shard_map/ppermute | solution.py:185
  14.6 1.5 %collective-permute-done.refs_1_ = f32[2,256,128]{2,1,0:T(8,128)S(1)} collective-permute-done((f32[2,256,128]{2,1,0:T(8,128)}, f32[2,256,128]{2,1,0:T(8,128)S(1)}, u32[]{:S(2)}, u32[]{:S(2)}) %collective-permute-start) | collective-permute-done | bytes 262176 | tf_op jit(solution)/shard_map/ppermute | solution.py:185
  16.1 0.2 collective-permute-start.5
  16.3 5.4 %collective-permute-done.1.refs_2_ = f32[2,256,128]{2,1,0:T(8,128)S(1)} collective-permute-done((f32[2,256,128]{2,1,0:T(8,128)}, f32[2,256,128]{2,1,0:T(8,128)S(1)}, u32[]{:S(2)}, u32[]{:S(2)}) %collective-permute-start.1) | collective-permute-done | bytes 262176 | tf_op jit(solution)/shard_map/ppermute | solution.py:185
  21.7 0.0 collective-permute-start.6
  21.7 27.3 %collective-permute-done.2.refs_3_ = f32[2,256,128]{2,1,0:T(8,128)S(1)} collective-permute-done((f32[2,256,128]{2,1,0:T(8,128)}, f32[2,256,128]{2,1,0:T(8,128)S(1)}, u32[]{:S(2)}, u32[]{:S(2)}) %collective-permute-start.2) | collective-permute-done | bytes 262176 | tf_op jit(solution)/shard_map/ppermute | solution.py:185
  49.0 5.6 %collective-permute-done.3.refs_4_ = f32[2,256,128]{2,1,0:T(8,128)S(1)} collective-permute-done((f32[2,256,128]{2,1,0:T(8,128)}, f32[2,256,128]{2,1,0:T(8,128)S(1)}, u32[]{:S(2)}, u32[]{:S(2)}) %collective-permute-start.3) | collective-permute-done | bytes 262176 | tf_op jit(solution)/shard_map/ppermute | solution.py:185
  54.6 0.0 collective-permute-done.4.refs_5_
  54.6 2.8 %collective-permute-done.5.refs_6_ = f32[2,256,128]{2,1,0:T(8,128)S(1)} collective-permute-done((f32[2,256,128]{2,1,0:T(8,128)}, f32[2,256,128]{2,1,0:T(8,128)S(1)}, u32[]{:S(2)}, u32[]{:S(2)}) %collective-permute-start.5) | collective-permute-done | bytes 262176 | tf_op jit(solution)/shard_map/ppermute | solution.py:185
  57.4 1.1 %collective-permute-done.6.refs_7_ = f32[2,256,128]{2,1,0:T(8,128)S(1)} collective-permute-done((f32[2,256,128]{2,1,0:T(8,128)}, f32[2,256,128]{2,1,0:T(8,128)S(1)}, u32[]{:S(2)}, u32[]{:S(2)}) %collective-permute-start.6) | collective-permute-done | bytes 262176 | tf_op jit(solution)/shard_map/ppermute | solution.py:185
  58.6 0.0 copy-done.1
  58.6 0.0 copy-done.2
  58.6 0.0 copy-done.3
  58.6 0.7 copy-done.7
  59.3 9.1 %shard_map.56 = (f32[2,1024,128]{2,1,0:T(8,128)}, f32[2,1024,128]{2,1,0:T(8,128)}) custom-call(s32[8]{0:T(128)} %order_ref.5, s32[8]{0:T(128)} %bits_ref.5, f32[2,256,128]{2,1,0:T(8,128)} %get-tuple-element.15.refs_0_, f32[2,256,128]{2,1,0:T(8,128)} %copy-done.1, f32[2,256,128]{2,1,0:T(8,128)} %copy-done.2, f32[2,256,128]{2,1,0:T(8,128)} %copy-done.3, ...), custom_call_target="tpu_custom_call" | custom-call | flops 1610612736 | bytes 4194304 | tf_op jit(solution)/shard_map/pallas_call | solution.py:153
  68.4 0.6 collective-permute-start.7
  69.0 2.5 %collective-permute-done.7.refs_1_ = f32[2,1024,128]{2,1,0:T(8,128)S(1)} collective-permute-done((f32[2,1024,128]{2,1,0:T(8,128)}, f32[2,1024,128]{2,1,0:T(8,128)S(1)}, u32[]{:S(2)}, u32[]{:S(2)}) %collective-permute-start.7) | collective-permute-done | bytes 1048608 | tf_op jit(solution)/shard_map/ppermute | solution.py:185
  71.5 1.0 %copy-done = f32[2,1024,128]{2,1,0:T(8,128)} copy-done((f32[2,1024,128]{2,1,0:T(8,128)}, f32[2,1024,128]{2,1,0:T(8,128)S(1)}, u32[]{:S(2)}) %copy-start) | copy-done | bytes 1048600
  72.5 7.3 %shard_map.57 = f32[4096,128]{1,0:T(8,128)} custom-call(s32[8]{0:T(128)} %order_ref.5, s32[8]{0:T(128)} %bits_ref.5, f32[2,1024,128]{2,1,0:T(8,128)} %get-tuple-element.23.refs_0_, f32[2,1024,128]{2,1,0:T(8,128)} %copy-done, bf16[8,2,128,128]{3,2,1,0:T(8,128)(2,1)} %refs_3_.3, bf16[8,2,128,128]{3,2,1,0:T(8,128)(2,1)} %refs_3_.3, f32[8,2,2,128]{3,2,1,0:T(2,128)} %refs_5_.3, ...), custom_call_target="tpu_custom_call" | custom-call | flops 1073741824 | bytes 4194304 | tf_op jit(solution)/shard_map/pallas_call | solution.py:153
  (11 shorter events, 0.0 us)
Async XLA Ops:
  8.7 7.5 %collective-permute-start = (f32[2,256,128]{2,1,0:T(8,128)}, f32[2,256,128]{2,1,0:T(8,128)S(1)}, u32[]{:S(2)}, u32[]{:S(2)}) collective-permute-start(f32[2,256,128]{2,1,0:T(8,128)} %get-tuple-element.16), channel_id=1, source_target_pairs={{0,2},{2,4},{4,6},{6,8},{8,10},{10,12},{12,14},{14,0},{1,3},{3,5},... | collective-permute-start | bytes 786440 | tf_op jit(solution)/shard_map/ppermute | solution.py:185
  10.0 11.7 %collective-permute-start.1 = (f32[2,256,128]{2,1,0:T(8,128)}, f32[2,256,128]{2,1,0:T(8,128)S(1)}, u32[]{:S(2)}, u32[]{:S(2)}) collective-permute-start(f32[2,256,128]{2,1,0:T(8,128)} %get-tuple-element.17), channel_id=1, source_target_pairs={{0,4},{2,6},{4,8},{6,10},{8,12},{10,14},{12,0},{14,2},{1,5},{3,7},... | collective-permute-start | bytes 786440 | tf_op jit(solution)/shard_map/ppermute | solution.py:185
  11.2 37.7 %collective-permute-start.2 = (f32[2,256,128]{2,1,0:T(8,128)}, f32[2,256,128]{2,1,0:T(8,128)S(1)}, u32[]{:S(2)}, u32[]{:S(2)}) collective-permute-start(f32[2,256,128]{2,1,0:T(8,128)} %get-tuple-element.18), channel_id=1, source_target_pairs={{0,6},{2,8},{4,10},{6,12},{8,14},{10,0},{12,2},{14,4},{1,7},{3,9},... | collective-permute-start | bytes 786440 | tf_op jit(solution)/shard_map/ppermute | solution.py:185
  12.2 42.4 %collective-permute-start.3 = (f32[2,256,128]{2,1,0:T(8,128)}, f32[2,256,128]{2,1,0:T(8,128)S(1)}, u32[]{:S(2)}, u32[]{:S(2)}) collective-permute-start(f32[2,256,128]{2,1,0:T(8,128)} %get-tuple-element.19), channel_id=1, source_target_pairs={{0,8},{2,10},{4,12},{6,14},{8,0},{10,2},{12,4},{14,6},{1,9},{3,11}... | collective-permute-start | bytes 786440 | tf_op jit(solution)/shard_map/ppermute | solution.py:185
  13.6 41.0 %collective-permute-start.4 = (f32[2,256,128]{2,1,0:T(8,128)}, f32[2,256,128]{2,1,0:T(8,128)S(1)}, u32[]{:S(2)}, u32[]{:S(2)}) collective-permute-start(f32[2,256,128]{2,1,0:T(8,128)} %get-tuple-element.20), channel_id=1, source_target_pairs={{0,10},{2,12},{4,14},{6,0},{8,2},{10,4},{12,6},{14,8},{1,11},{3,13... | collective-permute-start | bytes 786440 | tf_op jit(solution)/shard_map/ppermute | solution.py:185
  16.1 42.4 %copy-start.1 = (f32[2,256,128]{2,1,0:T(8,128)}, f32[2,256,128]{2,1,0:T(8,128)S(1)}, u32[]{:S(2)}) copy-start(f32[2,256,128]{2,1,0:T(8,128)S(1)} %collective-permute-done.refs_1_) | copy-start | bytes 786436
  16.1 41.3 %collective-permute-start.5 = (f32[2,256,128]{2,1,0:T(8,128)}, f32[2,256,128]{2,1,0:T(8,128)S(1)}, u32[]{:S(2)}, u32[]{:S(2)}) collective-permute-start(f32[2,256,128]{2,1,0:T(8,128)} %get-tuple-element.21), channel_id=1, source_target_pairs={{0,12},{2,14},{4,0},{6,2},{8,4},{10,6},{12,8},{14,10},{1,13},{3,15... | collective-permute-start | bytes 786440 | tf_op jit(solution)/shard_map/ppermute | solution.py:185
  21.7 36.9 %copy-start.2 = (f32[2,256,128]{2,1,0:T(8,128)}, f32[2,256,128]{2,1,0:T(8,128)S(1)}, u32[]{:S(2)}) copy-start(f32[2,256,128]{2,1,0:T(8,128)S(1)} %collective-permute-done.1.refs_2_) | copy-start | bytes 786436
  21.7 36.9 %collective-permute-start.6 = (f32[2,256,128]{2,1,0:T(8,128)}, f32[2,256,128]{2,1,0:T(8,128)S(1)}, u32[]{:S(2)}, u32[]{:S(2)}) collective-permute-start(f32[2,256,128]{2,1,0:T(8,128)} %get-tuple-element.22), channel_id=1, source_target_pairs={{0,14},{2,0},{4,2},{6,4},{8,6},{10,8},{12,10},{14,12},{1,15},{3,1}... | collective-permute-start | bytes 786440 | tf_op jit(solution)/shard_map/ppermute | solution.py:185
  49.0 9.6 %copy-start.3 = (f32[2,256,128]{2,1,0:T(8,128)}, f32[2,256,128]{2,1,0:T(8,128)S(1)}, u32[]{:S(2)}) copy-start(f32[2,256,128]{2,1,0:T(8,128)S(1)} %collective-permute-done.2.refs_3_) | copy-start | bytes 786436
  54.6 4.0 %copy-start.4 = (f32[2,256,128]{2,1,0:T(8,128)}, f32[2,256,128]{2,1,0:T(8,128)S(1)}, u32[]{:S(2)}) copy-start(f32[2,256,128]{2,1,0:T(8,128)S(1)} %collective-permute-done.3.refs_4_) | copy-start | bytes 786436
  54.6 4.0 %copy-start.5 = (f32[2,256,128]{2,1,0:T(8,128)}, f32[2,256,128]{2,1,0:T(8,128)S(1)}, u32[]{:S(2)}) copy-start(f32[2,256,128]{2,1,0:T(8,128)S(1)} %collective-permute-done.4.refs_5_) | copy-start | bytes 786436
  57.4 1.2 %copy-start.6 = (f32[2,256,128]{2,1,0:T(8,128)}, f32[2,256,128]{2,1,0:T(8,128)S(1)}, u32[]{:S(2)}) copy-start(f32[2,256,128]{2,1,0:T(8,128)S(1)} %collective-permute-done.5.refs_6_) | copy-start | bytes 786436
  58.6 0.7 copy-start.7
  68.4 3.1 %collective-permute-start.7 = (f32[2,1024,128]{2,1,0:T(8,128)}, f32[2,1024,128]{2,1,0:T(8,128)S(1)}, u32[]{:S(2)}, u32[]{:S(2)}) collective-permute-start(f32[2,1024,128]{2,1,0:T(8,128)} %get-tuple-element.24), channel_id=1, source_target_pairs={{0,1},{1,0},{2,3},{3,2},{4,5},{5,4},{6,7},{7,6},{8,9},{9,8},{10,11... | collective-permute-start | bytes 3145736 | tf_op jit(solution)/shard_map/ppermute | solution.py:185
  71.5 1.0 %copy-start = (f32[2,1024,128]{2,1,0:T(8,128)}, f32[2,1024,128]{2,1,0:T(8,128)S(1)}, u32[]{:S(2)}) copy-start(f32[2,1024,128]{2,1,0:T(8,128)S(1)} %collective-permute-done.7.refs_1_) | copy-start | bytes 3145732
where the time goes:
time: 80.1 us; the launch traced here: 79.8 us
  waiting for transfers between devices  46.3 us (58%)
  Pallas kernels  25.1 us (31%)
  starting transfers between devices  6.65 us (8%)
  local copies, waits for them, and re-layouts  1.68 us (2%)
    ppermute x8, waiting for transfers between devices, exchange(): lax.ppermute(pieces[k], axis, [(i, (i + k) % n) for i in range(n)])  46.3 us
    pallas_call x3, Pallas kernels, call(): pl.pallas_call(functools.partial(kernel, steps=steps, n_in=n_in, n_out=n_...  25.1 us
    ppermute x8, starting transfers between devices, exchange(): lax.ppermute(pieces[k], axis, [(i, (i + k) % n) for i in range(n)])  6.65 us
    unnamed x16, local copies, waits for them, and re-layouts  1.68 us
  transfers between devices with their start and end apart: 8, of which 7 were waited for; matrix products, arithmetic and copies ran while one was open for 0% of the time, Pallas kernels for 0%

commit v1 on v0

--- a/solution.py
+++ b/solution.py
@@ -6,6 +6,7 @@
 from jax.experimental import pallas as pl
 from jax.experimental.pallas import tpu as pltpu
 from jax.sharding import PartitionSpec as P
+
 
 UNROLL = 8
 
@@ -186,7 +187,7 @@
     ]
 
 
-def body(state, gates, bonds, order, bits):
+def general_body(state, gates, bonds, order, bits):
     dim = gates.shape[-1]
     rows = state.shape[1] // dim
     leading = lax.axis_size("outer")
@@ -201,6 +202,406 @@
     return flat.reshape(rows, 2, dim).transpose(1, 0, 2).reshape(2, rows * dim)
 
 
+VMEM_LIMIT = 20 * 2**20
+
+
+def gate_rows(gate_ref, scratch_ref, order):
+    for c in range(2):
+        scratch_ref[c] = gate_ref[c].astype(jnp.float32)
+    if order is None:
+        return [scratch_ref[c] for c in range(2)]
+    tall = scratch_ref.shape[1] // len(order)
+    return [
+        jnp.concatenate([scratch_ref[c, pl.ds(t, tall, stride=len(order)), :] for t in order], axis=0)
+        for c in range(2)
+    ]
+
+
+def make_weight(gate_ref, scratch_ref, weight_ref, order=None, halves=False):
+    real, imag = gate_rows(gate_ref, scratch_ref, order)
+    dim = real.shape[0]
+    cut = [(0, dim // 2), (dim // 2, dim)] if halves else [(0, dim)]
+    upper = [m[a:b] for a, b in cut for m in (real, imag)]
+    lower = [m[a:b] for a, b in cut for m in (-imag, real)]
+    weight_ref[:dim] = jnp.concatenate(upper, axis=0).T.astype(jnp.bfloat16)
+    weight_ref[dim:] = jnp.concatenate(lower, axis=0).T.astype(jnp.bfloat16)
+
+
+def apply_gate(load, store, weight_ref, bond_ref, groups, unroll):
+    bond_real = bond_ref[0:1, :]
+    bond_imag = bond_ref[1:2, :]
+
+    def some(index, carry):
+        high, low = [], []
+        for k in range(unroll):
+            tiles = load(index * unroll + k)
+            if len(tiles) == 1:
+                both = tiles[0].T
+                half = both.shape[0] // 2
+                real, imag = both[:half], both[half:]
+            else:
+                real, imag = tiles[0].T, tiles[1].T
+            scaled = jnp.concatenate(
+                [real * bond_real - imag * bond_imag, real * bond_imag + imag * bond_real], axis=1
+            )
+            head = scaled.astype(jnp.bfloat16)
+            high.append(head)
+            low.append((scaled - head.astype(jnp.float32)).astype(jnp.bfloat16))
+        product = jnp.dot(
+            jnp.concatenate(high + low, axis=0), weight_ref[...], preferred_element_type=jnp.float32
+        )
+        half = product.shape[0] // 2
+        product = product[:half] + product[half:]
+        size = half // unroll
+        for k in range(unroll):
+            store(index * unroll + k, product[k * size : (k + 1) * size])
+        return carry
+
+    lax.fori_loop(0, groups // unroll, some, 0)
+
+
+def tiles_of(ref, lead=()):
+    def load(g):
+        value = ref[(*lead, slice(None), pl.ds(pl.multiple_of(g * 8, 8), 8), slice(None))]
+        return value.reshape(-1, value.shape[-1])
+
+    return load
+
+
+def parts_of(ref):
+    loads = [tiles_of(ref, (c,)) for c in range(2)]
+    return lambda g: [load(g) for load in loads]
+
+
+def fetch(order_ref, bits_ref, first, gates_ref, bonds_ref, gate_buf, bond_buf, sem):
+    copies = []
+    for k in range(gate_buf.shape[0]):
+        which = order_ref[first + k]
+        copies.append(pltpu.make_async_copy(gates_ref.at[which], gate_buf.at[k], sem.at[k, 0]))
+        copies.append(
+            pltpu.make_async_copy(bonds_ref.at[which, bits_ref[first + k]], bond_buf.at[k], sem.at[k, 1])
+        )
+    for copy in copies:
+        copy.start()
+    return copies
+
+
+def start_all(copies):
+    for copy in copies:
+        copy.start()
+    return copies
+
+
+def wait_all(copies):
+    for copy in copies:
+        copy.wait()
+
+
+def second_third(half, d1, out_buf, outs, weights, bonds, sem):
+    groups = d1.shape[1]
+
+    def load(g):
+        return [half[pl.ds(g, half.shape[1], stride=groups), :]]
+
+    def store(g, value):
+        lanes = half.shape[1]
+        for c in range(2):
+            d1[c, g] = value[:, c * lanes : (c + 1) * lanes]
+
+    apply_gate(load, store, weights.at[0], bonds.at[0], groups, 8)
+    per = out_buf.shape[1] // len(outs)
+
+    def store_out(g, value):
+        lanes = half.shape[1]
+        for c in range(2):
+            out_buf[c, g] = value[:, c * lanes : (c + 1) * lanes]
+
+    apply_gate(parts_of(d1), store_out, weights.at[1], bonds.at[1], out_buf.shape[1], 8)
+    wait_all(
+        start_all(
+            [
+                pltpu.make_async_copy(out_buf.at[:, pl.ds(k * per, per)], outs[k], sem.at[k])
+                for k in range(len(outs))
+            ]
+        )
+    )
+
+
+def head_kernel(order_ref, bits_ref, x_ref, gates_ref, bonds_ref, *refs, n):
+    far_outs, near_ref = refs[: n // 2], refs[n // 2]
+    x_buf, far, near, d1, out_buf, gate_buf, bond_buf, gate_rows_buf, weights, g_sem, x_sem, o_sem, n_sem = refs[
+        n // 2 + 1 :
+    ]
+    groups = x_buf.shape[1]
+    me = lax.axis_index("outer")
+    gate_copies = fetch(order_ref, bits_ref, 0, gates_ref, bonds_ref, gate_buf, bond_buf, g_sem)
+
+    def x_copy(g, c):
+        return pltpu.make_async_copy(x_ref.at[:, g, c, :], x_buf.at[c, g], x_sem.at[c, g])
+
+    for g in range(groups):
+        for c in range(2):
+            x_copy(g, c).start()
+    wait_all(gate_copies)
+    rest = groups // n
+    leads = [(me ^ k) * rest + r for k in [*range(n // 2, n), *range(n // 2)] for r in range(rest)]
+    tiles = list(range(groups))
+    make_weight(gate_buf.at[0], gate_rows_buf, weights.at[0], leads, True)
+    make_weight(gate_buf.at[1], gate_rows_buf, weights.at[1], tiles)
+    make_weight(gate_buf.at[2], gate_rows_buf, weights.at[2], tiles, True)
+
+    def load(g):
+        for c in range(2):
+            x_copy(g, c).wait()
+        return [x_buf[c, g] for c in range(2)]
+
+    def store(g, value):
+        lanes = far.shape[1]
+        rows = pl.ds(pl.multiple_of(g * lanes, lanes), lanes)
+        far[rows, :] = value[:, :lanes]
+        near[rows, :] = value[:, lanes:]
+
+    apply_gate(load, store, weights.at[0], bond_buf.at[0], groups, 8)
+    near_copy = pltpu.make_async_copy(near, near_ref, n_sem)
+    near_copy.start()
+    second_third(far, d1, out_buf, far_outs, weights.at[pl.ds(1, 2)], bond_buf.at[pl.ds(1, 2)], o_sem)
+    near_copy.wait()
+
+
+def near_kernel(order_ref, bits_ref, near_ref, gates_ref, bonds_ref, *refs, n):
+    outs = refs[: n // 2]
+    near, d1, out_buf, gate_buf, bond_buf, gate_rows_buf, weights, g_sem, o_sem, n_sem = refs[n // 2 :]
+    near_copy = pltpu.make_async_copy(near_ref, near, n_sem)
+    near_copy.start()
+    wait_all(fetch(order_ref, bits_ref, 1, gates_ref, bonds_ref, gate_buf, bond_buf, g_sem))
+    tiles = list(range(d1.shape[1]))
+    make_weight(gate_buf.at[0], gate_rows_buf, weights.at[0], tiles)
+    make_weight(gate_buf.at[1], gate_rows_buf, weights.at[1], tiles, True)
+    near_copy.wait()
+    second_third(near, d1, out_buf, outs, weights, bond_buf, o_sem)
+
+
+def join_kernel(order_ref, bits_ref, gates_ref, bonds_ref, *refs, n):
+    ins, (own_ref, other_ref) = refs[:n], refs[n : n + 2]
+    v_buf, own, other, gate_buf, bond_buf, gate_rows_buf, weights, g_sem, i_sem, o_sem = refs[n + 2 :]
+    me = lax.axis_index("outer")
+    core = lax.axis_index("inner")
+    per = ins[0].shape[1]
+    copies = fetch(order_ref, bits_ref, 3, gates_ref, bonds_ref, gate_buf, bond_buf, g_sem)
+    in_copies = start_all(
+        [
+            pltpu.make_async_copy(ins[k], v_buf.at[:, pl.ds((me ^ k) * per, per)], i_sem.at[k])
+            for k in range(n)
+        ]
+    )
+    wait_all(copies)
+    groups = v_buf.shape[1]
+    leads = [(core ^ j) * (groups // 2) + r for j in range(2) for r in range(groups // 2)]
+    make_weight(gate_buf.at[0], gate_rows_buf, weights.at[0], leads, True)
+    wait_all(in_copies)
+    lanes = v_buf.shape[-1]
+    out_copies = []
+    for chunk in range(2):
+
+        def load(g):
+            return [tiles_of(v_buf, (chunk,))(g)]
+
+        def store(g, value):
+            own[chunk, g] = value[:, :lanes]
+            other[chunk, g] = value[:, lanes:]
+
+        apply_gate(load, store, weights.at[0], bond_buf.at[0], groups, 8)
+        out_copies += start_all(
+            [
+                pltpu.make_async_copy(other.at[chunk], other_ref.at[chunk], o_sem.at[1, chunk]),
+                pltpu.make_async_copy(own.at[chunk], own_ref.at[chunk], o_sem.at[0, chunk]),
+            ]
+        )
+    wait_all(out_copies)
+
+
+def fifth_sixth(q_buf, e_buf, s_buf, at, weights, bonds):
+    lanes = q_buf.shape[-1]
+    per = q_buf.shape[2] // 8
+    for chunk in range(2):
+
+        def load(g):
+            return [tiles_of(q_buf, (chunk,))(g)]
+
+        def store(g, value):
+            for c in range(2):
+                e_buf[c, chunk * per + g] = value[:, c * lanes : (c + 1) * lanes]
+
+        apply_gate(load, store, weights.at[0], bonds.at[0], per, per)
+
+    def store_s(g, value):
+        for c in range(2):
+            s_buf[c, at + g] = value[:, c * lanes : (c + 1) * lanes]
+
+    groups = e_buf.shape[2] // 8
+    apply_gate(parts_of(e_buf), store_s, weights.at[1], bonds.at[1], groups, groups)
+
+
+def own_kernel(order_ref, bits_ref, own_ref, gates_ref, bonds_ref, out_ref, *refs):
+    q_buf, e_buf, s_buf, gate_buf, bond_buf, gate_rows_buf, weights, g_sem, i_sem, o_sem = refs
+    copy = pltpu.make_async_copy(own_ref, q_buf, i_sem)
+    copy.start()
+    wait_all(fetch(order_ref, bits_ref, 4, gates_ref, bonds_ref, gate_buf, bond_buf, g_sem))
+    tiles = list(range(e_buf.shape[1]))
+    for k in range(2):
+        make_weight(gate_buf.at[k], gate_rows_buf, weights.at[k], tiles)
+    copy.wait()
+    fifth_sixth(q_buf, e_buf, s_buf, 0, weights, bond_buf)
+    copy = pltpu.make_async_copy(s_buf, out_ref, o_sem)
+    copy.start()
+    copy.wait()
+
+
+def tail_kernel(order_ref, bits_ref, done_ref, got_ref, gates_ref, bonds_ref, out_ref, *refs):
+    q_buf, e_buf, s_buf, f_buf, y_buf, gate_buf, bond_buf, gate_rows_buf, weights, g_sem, i_sem, y_sem = refs
+    core = lax.axis_index("inner")
+    half = s_buf.shape[1] // 2
+    got = pltpu.make_async_copy(got_ref, q_buf, i_sem.at[0])
+    got.start()
+    done = pltpu.make_async_copy(done_ref, s_buf.at[:, pl.ds(core * half, half)], i_sem.at[1])
+    done.start()
+    wait_all(fetch(order_ref, bits_ref, 4, gates_ref, bonds_ref, gate_buf, bond_buf, g_sem))
+    tiles = list(range(e_buf.shape[1]))
+    for k in range(4):
+        make_weight(gate_buf.at[k], gate_rows_buf, weights.at[k], tiles if k < 2 else None)
+    got.wait()
+    fifth_sixth(q_buf, e_buf, s_buf, (1 - core) * half, weights, bond_buf)
+    done.wait()
+    lanes = f_buf.shape[-1]
+    groups = f_buf.shape[1]
+
+    def store(g, value):
+        for c in range(2):
+            f_buf[c, g] = value[:, c * lanes : (c + 1) * lanes]
+
+    apply_gate(parts_of(s_buf), store, weights.at[2], bond_buf.at[2], groups, 8)
+
+    def y_copy(g, c):
+        return pltpu.make_async_copy(
+            y_buf.at[c, g], out_ref.at[pl.ds(pl.multiple_of(g * lanes, lanes), lanes), c, :], y_sem.at[c, g]
+        )
+
+    def store_y(g, value):
+        for c in range(2):
+            y_buf[c, g] = value[:, c * lanes : (c + 1) * lanes]
+            y_copy(g, c).start()
+
+    apply_gate(parts_of(f_buf), store_y, weights.at[3], bond_buf.at[3], groups, 8)
+    for g in range(groups):
+        for c in range(2):
+            y_copy(g, c).wait()
+
+
+def launch(body, scalars, ins, out_shape, scratch, steps, dim, work, limit=VMEM_LIMIT):
+    anywhere = pl.BlockSpec(memory_space=pl.ANY)
+    scratch, sems = scratch
+    common = [
+        pltpu.VMEM((steps, 2, dim, dim), jnp.bfloat16),
+        pltpu.VMEM((steps, 2, dim), jnp.float32),
+        pltpu.VMEM((2, dim, dim), jnp.float32),
+        pltpu.VMEM((steps, 2 * dim, 2 * dim), jnp.bfloat16),
+        pltpu.SemaphoreType.DMA((steps, 2)),
+    ]
+    return pl.pallas_call(
+        body,
+        out_shape=[jax.ShapeDtypeStruct(shape, jnp.float32) for shape in out_shape],
+        grid_spec=pltpu.PrefetchScalarGridSpec(
+            num_scalar_prefetch=2,
+            grid=(1,),
+            in_specs=[anywhere] * len(ins),
+            out_specs=[anywhere] * len(out_shape),
+            scratch_shapes=[pltpu.VMEM(shape, jnp.float32) for shape in scratch]
+            + common
+            + [pltpu.SemaphoreType.DMA(shape) for shape in sems],
+        ),
+        compiler_params=pltpu.CompilerParams(vmem_limit_bytes=limit),
+        cost_estimate=pl.CostEstimate(flops=work * 4 * dim**4, bytes_accessed=0, transcendentals=0),
+    )(*scalars, *ins)
+
+
+def swap(piece, axis, k):
+    n = lax.axis_size(axis)
+    return lax.ppermute(piece, axis, [(i, i ^ k) for i in range(n)])
+
+
+def fast_body(state, gates, bonds, order, bits):
+    dim = gates.shape[-1]
+    rows = state.shape[1] // dim
+    m = rows // dim
+    n = lax.axis_size("outer")
+    half = n // 2
+    scalars = (order, bits)
+    x = state.reshape(2, rows, dim).transpose(1, 0, 2).reshape(dim, m, 2, dim)
+    piece = (2, m // n, dim, dim)
+    block = (2, m, dim // 2, dim)
+    mids = [block, (2, m // 2, dim, dim)]
+    *far, near = launch(
+        functools.partial(head_kernel, n=n),
+        scalars,
+        (x, gates, bonds),
+        [piece] * half + [(rows, dim)],
+        ([(2, m, dim, dim), (rows, dim), (rows, dim)] + mids, [(2, m), (half,), ()]),
+        3,
+        dim,
+        8,
+        None,
+    )
+    sent = []
+    for k in range(half):
+        sent.append(swap(far[k], "outer", half + k))
+    far = sent
+    near = launch(
+        functools.partial(near_kernel, n=n),
+        scalars,
+        (near, gates, bonds),
+        [piece] * half,
+        ([(rows, dim)] + mids, [(half,), ()]),
+        2,
+        dim,
+        4,
+    )
+    near = [near[0]] + [swap(near[k], "outer", k) for k in range(1, half)]
+    own, other = launch(
+        functools.partial(join_kernel, n=n),
+        scalars,
+        (gates, bonds, *near, *far),
+        [block, block],
+        ([(2, m, dim, dim), block, block], [(n,), (2, 2)]),
+        1,
+        dim,
+        4,
+    )
+    got = swap(other, "inner", 1)
+    done = launch(
+        own_kernel, scalars, (own, gates, bonds), [mids[1]], ([block, block, mids[1]], [(), ()]), 2, dim, 4
+    )[0]
+    out = launch(
+        tail_kernel,
+        scalars,
+        (done, got, gates, bonds),
+        [(rows, 2, dim)],
+        ([block, block, (2, m, dim, dim), (2, m, dim, dim), (2, m, dim, dim)], [(2,), (2, m)]),
+        4,
+        dim,
+        12,
+    )[0]
+    return out.transpose(1, 0, 2).reshape(2, rows * dim)
+
+
+def body(state, gates, bonds, order, bits):
+    dim = gates.shape[-1]
+    m = state.shape[1] // dim // dim
+    n = lax.axis_size("outer")
+    if lax.axis_size("inner") == 2 and m * 8 == dim and m % n == 0:
+        return fast_body(state, gates, bonds, order, bits)
+    return general_body(state, gates, bonds, order, bits)
+
+
 def solution(mesh):
     in_specs = (P(None, ("parts", "outer", "inner")), P(), P(), P(), P("parts"))
     out_specs = P(None, ("parts", "outer", "inner"))

time: 80.1 us -> 75.8 us (0.946)
  the two profiles are of different devices: /device:TPU:13 before, /device:TPU:19 now
where the time goes in v1:
time: 75.8 us; the launch traced here: 75.5 us
  waiting for transfers between devices  44.3 us (58%)
  Pallas kernels  21.4 us (28%)
  starting transfers between devices  8.54 us (11%)
  local copies, waits for them, and re-layouts  1.25 us (2%)
    ppermute x8, waiting for transfers between devices, swap(): return lax.ppermute(piece, axis, [(i, i ^ k) for i in range(n)])  44.3 us
    pallas_call x5, Pallas kernels, launch(): pl.pallas_call(body, out_shape=[jax.ShapeDtypeStruct(shape, jnp.float32)...  21.4 us
    ppermute x8, starting transfers between devices, swap(): return lax.ppermute(piece, axis, [(i, i ^ k) for i in range(n)])  8.54 us
  transfers between devices with their start and end apart: 8, of which 6 were waited for; matrix products, arithmetic and copies ran while one was open for 0% of the time, Pallas kernels for 3%

profile of v1, /device:TPU:19, one launch (start us, length us, event | category | flops | bytes accessed | tf_op | source)
XLA Modules:
  0.0 75.5 jit_solution(10088245035061574105)
XLA Ops:
  0.0 7.9 %shard_map.55 = (f32[2,2,128,128]{3,2,1,0:T(8,128)}, f32[2,2,128,128]{3,2,1,0:T(8,128)}, f32[2,2,128,128]{3,2,1,0:T(8,128)}, f32[2,2,128,128]{3,2,1,0:T(8,128)}, f32[2048,128]{1,0:T(8,128)}) custom-call(s32[8]{0:T(128)} %order_ref.9, s32[8]{0:T(128)} %bits_ref.9, f32[128,16,2,128]{3,2,1,0:T(2,128)} %bitcast.8, bf16[8,2,128,128]{3,2,1,0:T(8,128)(2,1)} %gates_ref.9, ...), custom_call_target="tpu_custom_call" | custom-call | flops 8589934592 | tf_op jit(solution)/shard_map/pallas_call | solution.py:510
  8.0 0.0 copy-start.4
  8.0 1.2 %copy-done.4 = f32[2048,128]{1,0:T(8,128)S(1)} copy-done((f32[2048,128]{1,0:T(8,128)S(1)}, f32[2048,128]{1,0:T(8,128)}, u32[]{:S(2)}) %copy-start.4) | copy-done | bytes 1048600
  9.2 2.4 %shard_map.56 = (f32[2,2,128,128]{3,2,1,0:T(8,128)S(1)}, f32[2,2,128,128]{3,2,1,0:T(8,128)S(1)}, f32[2,2,128,128]{3,2,1,0:T(8,128)S(1)}, f32[2,2,128,128]{3,2,1,0:T(8,128)S(1)}) custom-call(s32[8]{0:T(128)S(1)} %copy-done.2, s32[8]{0:T(128)S(1)} %copy-done.3, f32[2048,128]{1,0:T(8,128)S(1)} %copy-done.4, bf16[8,2,128,128]{3,2,1,0:T(8,128)(2,1)S(1)} %copy-done, ...), custom_call_target="tpu_custom_call" | custom-call | flops 4294967296 | tf_op jit(solution)/shard_map/pallas_call | solution.py:510
  11.6 1.3 %collective-permute-start = (f32[2,2,128,128]{3,2,1,0:T(8,128)S(1)}, f32[2,2,128,128]{3,2,1,0:T(8,128)S(1)}, u32[]{:S(2)}, u32[]{:S(2)}) collective-permute-start(f32[2,2,128,128]{3,2,1,0:T(8,128)S(1)} %get-tuple-element.18), channel_id=1, source_target_pairs={{0,2},{2,0},{4,6},{6,4},{8,10},{10,8},{12,14},{14,12},{1,3},{3,1},... | collective-permute-start | bytes 786440 | tf_op jit(solution)/shard_map/ppermute | solution.py:529
  12.9 1.3 %collective-permute-start.1 = (f32[2,2,128,128]{3,2,1,0:T(8,128)S(1)}, f32[2,2,128,128]{3,2,1,0:T(8,128)S(1)}, u32[]{:S(2)}, u32[]{:S(2)}) collective-permute-start(f32[2,2,128,128]{3,2,1,0:T(8,128)S(1)} %get-tuple-element.19), channel_id=1, source_target_pairs={{0,4},{2,6},{4,0},{6,2},{8,12},{10,14},{12,8},{14,10},{1,5},{3,7},... | collective-permute-start | bytes 786440 | tf_op jit(solution)/shard_map/ppermute | solution.py:529
  14.2 0.1 collective-permute-start.2
  14.4 0.0 copy-done.8
  14.4 0.1 collective-permute-start.3
  14.4 3.2 %collective-permute-start.4 = (f32[2,2,128,128]{3,2,1,0:T(8,128)S(1)}, f32[2,2,128,128]{3,2,1,0:T(8,128)S(1)}, u32[]{:S(2)}, u32[]{:S(2)}) collective-permute-start(f32[2,2,128,128]{3,2,1,0:T(8,128)S(1)} %copy-done.7), channel_id=1, source_target_pairs={{0,10},{2,8},{4,14},{6,12},{8,2},{10,0},{12,6},{14,4},{1,11},{3,9}... | collective-permute-start | bytes 786440 | tf_op jit(solution)/shard_map/ppermute | solution.py:529
  17.7 1.2 %collective-permute-done.refs_1_ = f32[2,2,128,128]{3,2,1,0:T(8,128)S(1)} collective-permute-done((f32[2,2,128,128]{3,2,1,0:T(8,128)S(1)}, f32[2,2,128,128]{3,2,1,0:T(8,128)S(1)}, u32[]{:S(2)}, u32[]{:S(2)}) %collective-permute-start) | collective-permute-done | bytes 262176 | tf_op jit(solution)/shard_map/ppermute | solution.py:529
  18.9 0.1 collective-permute-start.5
  19.0 8.5 %collective-permute-done.1.refs_2_ = f32[2,2,128,128]{3,2,1,0:T(8,128)S(1)} collective-permute-done((f32[2,2,128,128]{3,2,1,0:T(8,128)S(1)}, f32[2,2,128,128]{3,2,1,0:T(8,128)S(1)}, u32[]{:S(2)}, u32[]{:S(2)}) %collective-permute-start.1) | collective-permute-done | bytes 262176 | tf_op jit(solution)/shard_map/ppermute | solution.py:529
  27.6 0.0 collective-permute-start.6
  27.6 5.8 %collective-permute-done.2.refs_3_ = f32[2,2,128,128]{3,2,1,0:T(8,128)S(1)} collective-permute-done((f32[2,2,128,128]{3,2,1,0:T(8,128)S(1)}, f32[2,2,128,128]{3,2,1,0:T(8,128)S(1)}, u32[]{:S(2)}, u32[]{:S(2)}) %collective-permute-start.2) | collective-permute-done | bytes 262176 | tf_op jit(solution)/shard_map/ppermute | solution.py:529
  33.3 0.0 collective-permute-done.3.refs_4_
  33.3 3.2 %collective-permute-done.4.refs_5_ = f32[2,2,128,128]{3,2,1,0:T(8,128)S(1)} collective-permute-done((f32[2,2,128,128]{3,2,1,0:T(8,128)S(1)}, f32[2,2,128,128]{3,2,1,0:T(8,128)S(1)}, u32[]{:S(2)}, u32[]{:S(2)}) %collective-permute-start.4) | collective-permute-done | bytes 262176 | tf_op jit(solution)/shard_map/ppermute | solution.py:529
  36.6 19.0 %collective-permute-done.5.refs_6_ = f32[2,2,128,128]{3,2,1,0:T(8,128)S(1)} collective-permute-done((f32[2,2,128,128]{3,2,1,0:T(8,128)S(1)}, f32[2,2,128,128]{3,2,1,0:T(8,128)S(1)}, u32[]{:S(2)}, u32[]{:S(2)}) %collective-permute-start.5) | collective-permute-done | bytes 262176 | tf_op jit(solution)/shard_map/ppermute | solution.py:529
  55.5 6.6 %collective-permute-done.6.refs_7_ = f32[2,2,128,128]{3,2,1,0:T(8,128)S(1)} collective-permute-done((f32[2,2,128,128]{3,2,1,0:T(8,128)S(1)}, f32[2,2,128,128]{3,2,1,0:T(8,128)S(1)}, u32[]{:S(2)}, u32[]{:S(2)}) %collective-permute-start.6) | collective-permute-done | bytes 262176 | tf_op jit(solution)/shard_map/ppermute | solution.py:529
  62.1 2.7 %shard_map.57 = (f32[2,16,64,128]{3,2,1,0:T(8,128)S(1)}, f32[2,16,64,128]{3,2,1,0:T(8,128)S(1)}) custom-call(s32[8]{0:T(128)S(1)} %copy-done.2, s32[8]{0:T(128)S(1)} %copy-done.3, bf16[8,2,128,128]{3,2,1,0:T(8,128)(2,1)S(1)} %copy-done, f32[8,2,2,128]{3,2,1,0:T(2,128)S(1)} %copy-done.1, f32[2,2,128,128]{3,2,1,0:T(8,128)S(1)} %get-tuple-element.17.refs_0_, ...), custom_call_target="tpu_custom_call" | custom-call | flops 4294967296 | tf_op jit(solution)/shard_map/pallas_call | solution.py:510
  64.8 2.4 %collective-permute-start.7 = (f32[2,16,64,128]{3,2,1,0:T(8,128)S(1)}, f32[2,16,64,128]{3,2,1,0:T(8,128)S(1)}, u32[]{:S(2)}, u32[]{:S(2)}) collective-permute-start(f32[2,16,64,128]{3,2,1,0:T(8,128)S(1)} %get-tuple-element.26), channel_id=1, source_target_pairs={{0,1},{1,0},{2,3},{3,2},{4,5},{5,4},{6,7},{7,6},{8,9},{9,8},{10,11... | collective-permute-start | bytes 3145736 | tf_op jit(solution)/shard_map/ppermute | solution.py:529
  67.2 2.5 %shard_map.58.done_ref = f32[2,8,128,128]{3,2,1,0:T(8,128)S(1)} custom-call(s32[8]{0:T(128)S(1)} %copy-done.2, s32[8]{0:T(128)S(1)} %copy-done.3, f32[2,16,64,128]{3,2,1,0:T(8,128)S(1)} %get-tuple-element.25.own_ref, bf16[8,2,128,128]{3,2,1,0:T(8,128)(2,1)S(1)} %copy-done, f32[8,2,2,128]{3,2,1,0:T(2,128)S(1)} %copy-done.1), custom_call_target="tpu_custom_call" | custom-call | flops 4294967296 | tf_op jit(solution)/shard_map/pallas_call | solution.py:510
  69.7 0.0 collective-permute-done.7.got_ref
  69.7 5.8 %shard_map.59 = f32[2048,2,128]{2,1,0:T(2,128)} custom-call(s32[8]{0:T(128)S(1)} %copy-done.2, s32[8]{0:T(128)S(1)} %copy-done.3, f32[2,8,128,128]{3,2,1,0:T(8,128)S(1)} %shard_map.58.done_ref, f32[2,16,64,128]{3,2,1,0:T(8,128)S(1)} %collective-permute-done.7.got_ref, bf16[8,2,128,128]{3,2,1,0:T(8,128)(2,1)S(1)} %copy-done, f32[8,2,2,128]{3,2,1,0:T(2,128)S(1)} %copy-done.1), custom_call_target="tpu_custom_call" | custom-call | flops 12884901888 | tf_op jit(solution)/shard_map/pallas_call | solution.py:510
  (15 shorter events, 0.0 us)
Async XLA Ops:
  0.0 7.9 %copy-start = (bf16[8,2,128,128]{3,2,1,0:T(8,128)(2,1)S(1)}, bf16[8,2,128,128]{3,2,1,0:T(8,128)(2,1)}, u32[]{:S(2)}) copy-start(bf16[8,2,128,128]{3,2,1,0:T(8,128)(2,1)} %gates_ref.9) | copy-start | bytes 1572868
  0.0 7.9 %copy-start.1 = (f32[8,2,2,128]{3,2,1,0:T(2,128)S(1)}, f32[8,2,2,128]{3,2,1,0:T(2,128)}, u32[]{:S(2)}) copy-start(f32[8,2,2,128]{3,2,1,0:T(2,128)} %bonds_ref.9) | copy-start | bytes 49156
  0.0 8.0 %copy-start.2 = (s32[8]{0:T(128)S(1)}, s32[8]{0:T(128)}, u32[]{:S(2)}) copy-start(s32[8]{0:T(128)} %order_ref.9) | copy-start | bytes 100
  0.0 8.0 %copy-start.3 = (s32[8]{0:T(128)S(1)}, s32[8]{0:T(128)}, u32[]{:S(2)}) copy-start(s32[8]{0:T(128)} %bits_ref.9) | copy-start | bytes 100
  8.0 1.2 %copy-start.4 = (f32[2048,128]{1,0:T(8,128)S(1)}, f32[2048,128]{1,0:T(8,128)}, u32[]{:S(2)}) copy-start(f32[2048,128]{1,0:T(8,128)} %get-tuple-element.16.near_ref) | copy-start | bytes 3145732
  9.2 5.2 %copy-start.8 = (f32[2,2,128,128]{3,2,1,0:T(8,128)S(1)}, f32[2,2,128,128]{3,2,1,0:T(8,128)}, u32[]{:S(2)}) copy-start(f32[2,2,128,128]{3,2,1,0:T(8,128)} %get-tuple-element.21) | copy-start | bytes 786436
  9.2 5.2 %copy-start.7 = (f32[2,2,128,128]{3,2,1,0:T(8,128)S(1)}, f32[2,2,128,128]{3,2,1,0:T(8,128)}, u32[]{:S(2)}) copy-start(f32[2,2,128,128]{3,2,1,0:T(8,128)} %get-tuple-element.22) | copy-start | bytes 786436
  9.2 9.7 %copy-start.6 = (f32[2,2,128,128]{3,2,1,0:T(8,128)S(1)}, f32[2,2,128,128]{3,2,1,0:T(8,128)}, u32[]{:S(2)}) copy-start(f32[2,2,128,128]{3,2,1,0:T(8,128)} %get-tuple-element.23) | copy-start | bytes 786436
  9.2 18.4 %copy-start.5 = (f32[2,2,128,128]{3,2,1,0:T(8,128)S(1)}, f32[2,2,128,128]{3,2,1,0:T(8,128)}, u32[]{:S(2)}) copy-start(f32[2,2,128,128]{3,2,1,0:T(8,128)} %get-tuple-element.24) | copy-start | bytes 786436
  11.6 7.3 %collective-permute-start = (f32[2,2,128,128]{3,2,1,0:T(8,128)S(1)}, f32[2,2,128,128]{3,2,1,0:T(8,128)S(1)}, u32[]{:S(2)}, u32[]{:S(2)}) collective-permute-start(f32[2,2,128,128]{3,2,1,0:T(8,128)S(1)} %get-tuple-element.18), channel_id=1, source_target_pairs={{0,2},{2,0},{4,6},{6,4},{8,10},{10,8},{12,14},{14,12},{1,3},{3,1},... | collective-permute-start | bytes 786440 | tf_op jit(solution)/shard_map/ppermute | solution.py:529
  12.9 14.6 %collective-permute-start.1 = (f32[2,2,128,128]{3,2,1,0:T(8,128)S(1)}, f32[2,2,128,128]{3,2,1,0:T(8,128)S(1)}, u32[]{:S(2)}, u32[]{:S(2)}) collective-permute-start(f32[2,2,128,128]{3,2,1,0:T(8,128)S(1)} %get-tuple-element.19), channel_id=1, source_target_pairs={{0,4},{2,6},{4,0},{6,2},{8,12},{10,14},{12,8},{14,10},{1,5},{3,7},... | collective-permute-start | bytes 786440 | tf_op jit(solution)/shard_map/ppermute | solution.py:529
  14.2 19.1 %collective-permute-start.2 = (f32[2,2,128,128]{3,2,1,0:T(8,128)S(1)}, f32[2,2,128,128]{3,2,1,0:T(8,128)S(1)}, u32[]{:S(2)}, u32[]{:S(2)}) collective-permute-start(f32[2,2,128,128]{3,2,1,0:T(8,128)S(1)} %get-tuple-element.20), channel_id=1, source_target_pairs={{0,6},{2,4},{4,2},{6,0},{8,14},{10,12},{12,10},{14,8},{1,7},{3,5},... | collective-permute-start | bytes 786440 | tf_op jit(solution)/shard_map/ppermute | solution.py:529
  14.4 19.0 %collective-permute-start.3 = (f32[2,2,128,128]{3,2,1,0:T(8,128)S(1)}, f32[2,2,128,128]{3,2,1,0:T(8,128)S(1)}, u32[]{:S(2)}, u32[]{:S(2)}) collective-permute-start(f32[2,2,128,128]{3,2,1,0:T(8,128)S(1)} %copy-done.8), channel_id=1, source_target_pairs={{0,8},{2,10},{4,12},{6,14},{8,0},{10,2},{12,4},{14,6},{1,9},{3,11}... | collective-permute-start | bytes 786440 | tf_op jit(solution)/shard_map/ppermute | solution.py:529
  14.4 22.1 %collective-permute-start.4 = (f32[2,2,128,128]{3,2,1,0:T(8,128)S(1)}, f32[2,2,128,128]{3,2,1,0:T(8,128)S(1)}, u32[]{:S(2)}, u32[]{:S(2)}) collective-permute-start(f32[2,2,128,128]{3,2,1,0:T(8,128)S(1)} %copy-done.7), channel_id=1, source_target_pairs={{0,10},{2,8},{4,14},{6,12},{8,2},{10,0},{12,6},{14,4},{1,11},{3,9}... | collective-permute-start | bytes 786440 | tf_op jit(solution)/shard_map/ppermute | solution.py:529
  18.9 36.6 %collective-permute-start.5 = (f32[2,2,128,128]{3,2,1,0:T(8,128)S(1)}, f32[2,2,128,128]{3,2,1,0:T(8,128)S(1)}, u32[]{:S(2)}, u32[]{:S(2)}) collective-permute-start(f32[2,2,128,128]{3,2,1,0:T(8,128)S(1)} %copy-done.6), channel_id=1, source_target_pairs={{0,12},{2,14},{4,8},{6,10},{8,4},{10,6},{12,0},{14,2},{1,13},{3,15... | collective-permute-start | bytes 786440 | tf_op jit(solution)/shard_map/ppermute | solution.py:529
  27.6 34.5 %collective-permute-start.6 = (f32[2,2,128,128]{3,2,1,0:T(8,128)S(1)}, f32[2,2,128,128]{3,2,1,0:T(8,128)S(1)}, u32[]{:S(2)}, u32[]{:S(2)}) collective-permute-start(f32[2,2,128,128]{3,2,1,0:T(8,128)S(1)} %copy-done.5), channel_id=1, source_target_pairs={{0,14},{2,12},{4,10},{6,8},{8,6},{10,4},{12,2},{14,0},{1,15},{3,13... | collective-permute-start | bytes 786440 | tf_op jit(solution)/shard_map/ppermute | solution.py:529
  64.8 4.9 %collective-permute-start.7 = (f32[2,16,64,128]{3,2,1,0:T(8,128)S(1)}, f32[2,16,64,128]{3,2,1,0:T(8,128)S(1)}, u32[]{:S(2)}, u32[]{:S(2)}) collective-permute-start(f32[2,16,64,128]{3,2,1,0:T(8,128)S(1)} %get-tuple-element.26), channel_id=1, source_target_pairs={{0,1},{1,0},{2,3},{3,2},{4,5},{5,4},{6,7},{7,6},{8,9},{9,8},{10,11... | collective-permute-start | bytes 3145736 | tf_op jit(solution)/shard_map/ppermute | solution.py:529

commit v2 on v1

--- a/solution.py
+++ b/solution.py
@@ -202,6 +202,8 @@
     return flat.reshape(rows, 2, dim).transpose(1, 0, 2).reshape(2, rows * dim)
 
 
+DOT_ROWS = 128
+TAIL_BATCHES = 2
 VMEM_LIMIT = 20 * 2**20
 
 
@@ -217,8 +219,19 @@
     ]
 
 
-def make_weight(gate_ref, scratch_ref, weight_ref, order=None, halves=False):
+def swap_lanes(value, amount, steps):
+    lane = lax.broadcasted_iota(jnp.int32, value.shape, 1)
+    size = value.shape[1]
+    for s in steps:
+        other = jnp.where((lane & s) != 0, pltpu.roll(value, s, 1), pltpu.roll(value, size - s, 1))
+        value = jnp.where((amount & s) != 0, other, value)
+    return value
+
+
+def make_weight(gate_ref, scratch_ref, weight_ref, order=None, halves=False, lanes=None):
     real, imag = gate_rows(gate_ref, scratch_ref, order)
+    if lanes is not None:
+        real, imag = swap_lanes(real, *lanes), swap_lanes(imag, *lanes)
     dim = real.shape[0]
     cut = [(0, dim // 2), (dim // 2, dim)] if halves else [(0, dim)]
     upper = [m[a:b] for a, b in cut for m in (real, imag)]
@@ -227,14 +240,16 @@
     weight_ref[dim:] = jnp.concatenate(lower, axis=0).T.astype(jnp.bfloat16)
 
 
-def apply_gate(load, store, weight_ref, bond_ref, groups, unroll):
+def apply_gate(load, store, weight_ref, bond_ref, groups, before=None, after=None, batch=None):
     bond_real = bond_ref[0:1, :]
     bond_imag = bond_ref[1:2, :]
-
-    def some(index, carry):
-        high, low = [], []
-        for k in range(unroll):
-            tiles = load(index * unroll + k)
+    batch = batch or groups
+    for first in range(0, groups, batch):
+        if before is not None:
+            before(range(first, first + batch))
+        held = []
+        for g in range(first, first + batch):
+            tiles = load(g)
             if len(tiles) == 1:
                 both = tiles[0].T
                 half = both.shape[0] // 2
@@ -245,24 +260,24 @@
                 [real * bond_real - imag * bond_imag, real * bond_imag + imag * bond_real], axis=1
             )
             head = scaled.astype(jnp.bfloat16)
-            high.append(head)
-            low.append((scaled - head.astype(jnp.float32)).astype(jnp.bfloat16))
-        product = jnp.dot(
-            jnp.concatenate(high + low, axis=0), weight_ref[...], preferred_element_type=jnp.float32
-        )
-        half = product.shape[0] // 2
-        product = product[:half] + product[half:]
-        size = half // unroll
-        for k in range(unroll):
-            store(index * unroll + k, product[k * size : (k + 1) * size])
-        return carry
-
-    lax.fori_loop(0, groups // unroll, some, 0)
+            held.append((g, head, (scaled - head.astype(jnp.float32)).astype(jnp.bfloat16)))
+            rows = scaled.shape[0]
+            if rows * len(held) < DOT_ROWS and g + 1 < first + batch:
+                continue
+            lhs = jnp.concatenate([h for _, h, _ in held] + [l for _, _, l in held], axis=0)
+            product = jnp.dot(lhs, weight_ref[...], preferred_element_type=jnp.float32)
+            half = product.shape[0] // 2
+            product = product[:half] + product[half:]
+            for k, (at, _, _) in enumerate(held):
+                store(at, product[k * rows : (k + 1) * rows])
+            held = []
+        if after is not None:
+            after(range(first, first + batch))
 
 
 def tiles_of(ref, lead=()):
     def load(g):
-        value = ref[(*lead, slice(None), pl.ds(pl.multiple_of(g * 8, 8), 8), slice(None))]
+        value = ref[(*lead, slice(None), pl.ds(g * 8, 8), slice(None))]
         return value.reshape(-1, value.shape[-1])
 
     return load
@@ -297,40 +312,31 @@
         copy.wait()
 
 
-def second_third(half, d1, out_buf, outs, weights, bonds, sem):
+def second_third(half, d1, out_buf, targets, weights, bonds):
     groups = d1.shape[1]
+    lanes = half.shape[1]
 
     def load(g):
-        return [half[pl.ds(g, half.shape[1], stride=groups), :]]
+        return [half[pl.ds(g, lanes, stride=groups), :]]
 
     def store(g, value):
-        lanes = half.shape[1]
         for c in range(2):
             d1[c, g] = value[:, c * lanes : (c + 1) * lanes]
 
-    apply_gate(load, store, weights.at[0], bonds.at[0], groups, 8)
-    per = out_buf.shape[1] // len(outs)
+    apply_gate(load, store, weights.at[0], bonds.at[0], groups)
 
     def store_out(g, value):
-        lanes = half.shape[1]
         for c in range(2):
             out_buf[c, g] = value[:, c * lanes : (c + 1) * lanes]
 
-    apply_gate(parts_of(d1), store_out, weights.at[1], bonds.at[1], out_buf.shape[1], 8)
-    wait_all(
-        start_all(
-            [
-                pltpu.make_async_copy(out_buf.at[:, pl.ds(k * per, per)], outs[k], sem.at[k])
-                for k in range(len(outs))
-            ]
-        )
-    )
+    apply_gate(parts_of(d1), store_out, weights.at[1], bonds.at[1], out_buf.shape[1])
+    wait_all(start_all(targets))
 
 
 def head_kernel(order_ref, bits_ref, x_ref, gates_ref, bonds_ref, *refs, n):
-    far_outs, near_ref = refs[: n // 2], refs[n // 2]
+    far_outs, near_ref = refs[:n], refs[n]
     x_buf, far, near, d1, out_buf, gate_buf, bond_buf, gate_rows_buf, weights, g_sem, x_sem, o_sem, n_sem = refs[
-        n // 2 + 1 :
+        n + 1 :
     ]
     groups = x_buf.shape[1]
     me = lax.axis_index("outer")
@@ -351,20 +357,26 @@
     make_weight(gate_buf.at[2], gate_rows_buf, weights.at[2], tiles, True)
 
     def load(g):
-        for c in range(2):
-            x_copy(g, c).wait()
         return [x_buf[c, g] for c in range(2)]
+
+    def arrive(some):
+        wait_all([x_copy(g, c) for g in some for c in range(2)])
 
     def store(g, value):
         lanes = far.shape[1]
-        rows = pl.ds(pl.multiple_of(g * lanes, lanes), lanes)
+        rows = pl.ds(g * lanes, lanes)
         far[rows, :] = value[:, :lanes]
         near[rows, :] = value[:, lanes:]
 
-    apply_gate(load, store, weights.at[0], bond_buf.at[0], groups, 8)
+    apply_gate(load, store, weights.at[0], bond_buf.at[0], groups, before=arrive)
     near_copy = pltpu.make_async_copy(near, near_ref, n_sem)
     near_copy.start()
-    second_third(far, d1, out_buf, far_outs, weights.at[pl.ds(1, 2)], bond_buf.at[pl.ds(1, 2)], o_sem)
+    targets = [
+        pltpu.make_async_copy(out_buf.at[chunk, pl.ds(k * rest, rest)], far_outs[2 * k + chunk], o_sem.at[k, chunk])
+        for chunk in range(2)
+        for k in range(n // 2)
+    ]
+    second_third(far, d1, out_buf, targets, weights.at[pl.ds(1, 2)], bond_buf.at[pl.ds(1, 2)])
     near_copy.wait()
 
 
@@ -378,123 +390,121 @@
     make_weight(gate_buf.at[0], gate_rows_buf, weights.at[0], tiles)
     make_weight(gate_buf.at[1], gate_rows_buf, weights.at[1], tiles, True)
     near_copy.wait()
-    second_third(near, d1, out_buf, outs, weights, bond_buf, o_sem)
-
-
-def join_kernel(order_ref, bits_ref, gates_ref, bonds_ref, *refs, n):
-    ins, (own_ref, other_ref) = refs[:n], refs[n : n + 2]
-    v_buf, own, other, gate_buf, bond_buf, gate_rows_buf, weights, g_sem, i_sem, o_sem = refs[n + 2 :]
+    rest = d1.shape[1] // n
+    targets = [
+        pltpu.make_async_copy(out_buf.at[:, pl.ds(k * rest, rest)], outs[k], o_sem.at[k]) for k in range(n // 2)
+    ]
+    second_third(near, d1, out_buf, targets, weights, bond_buf)
+
+
+def prep_kernel(order_ref, bits_ref, gates_ref, bonds_ref, weights, bonds, gate_buf, bond_buf, gate_rows_buf, g_sem, *, n):
     me = lax.axis_index("outer")
     core = lax.axis_index("inner")
-    per = ins[0].shape[1]
-    copies = fetch(order_ref, bits_ref, 3, gates_ref, bonds_ref, gate_buf, bond_buf, g_sem)
-    in_copies = start_all(
-        [
-            pltpu.make_async_copy(ins[k], v_buf.at[:, pl.ds((me ^ k) * per, per)], i_sem.at[k])
-            for k in range(n)
-        ]
-    )
-    wait_all(copies)
-    groups = v_buf.shape[1]
+    wait_all(fetch(order_ref, bits_ref, 3, gates_ref, bonds_ref, gate_buf, bond_buf, g_sem))
+    dim = gate_rows_buf.shape[-1]
+    groups = dim // 8
+    tiles = list(range(groups))
     leads = [(core ^ j) * (groups // 2) + r for j in range(2) for r in range(groups // 2)]
-    make_weight(gate_buf.at[0], gate_rows_buf, weights.at[0], leads, True)
-    wait_all(in_copies)
-    lanes = v_buf.shape[-1]
-    out_copies = []
-    for chunk in range(2):
-
-        def load(g):
-            return [tiles_of(v_buf, (chunk,))(g)]
-
-        def store(g, value):
-            own[chunk, g] = value[:, :lanes]
-            other[chunk, g] = value[:, lanes:]
-
-        apply_gate(load, store, weights.at[0], bond_buf.at[0], groups, 8)
-        out_copies += start_all(
-            [
-                pltpu.make_async_copy(other.at[chunk], other_ref.at[chunk], o_sem.at[1, chunk]),
-                pltpu.make_async_copy(own.at[chunk], own_ref.at[chunk], o_sem.at[0, chunk]),
-            ]
-        )
-    wait_all(out_copies)
-
-
-def fifth_sixth(q_buf, e_buf, s_buf, at, weights, bonds):
-    lanes = q_buf.shape[-1]
-    per = q_buf.shape[2] // 8
-    for chunk in range(2):
-
-        def load(g):
-            return [tiles_of(q_buf, (chunk,))(g)]
-
-        def store(g, value):
-            for c in range(2):
-                e_buf[c, chunk * per + g] = value[:, c * lanes : (c + 1) * lanes]
-
-        apply_gate(load, store, weights.at[0], bonds.at[0], per, per)
-
-    def store_s(g, value):
+    part = dim // n
+    joined = (me * part, [part << i for i in range((n - 1).bit_length())])
+    cored = (core * (dim // 2), [dim // 2])
+    make_weight(gate_buf.at[0], gate_rows_buf, weights.at[0], leads, True, joined)
+    make_weight(gate_buf.at[1], gate_rows_buf, weights.at[1], tiles)
+    make_weight(gate_buf.at[2], gate_rows_buf, weights.at[2], tiles)
+    make_weight(gate_buf.at[3], gate_rows_buf, weights.at[3], None, False, cored)
+    make_weight(gate_buf.at[4], gate_rows_buf, weights.at[4])
+    for k, lanes in enumerate([joined, None, None, cored, None]):
+        bonds[k] = bond_buf[k] if lanes is None else swap_lanes(bond_buf[k], *lanes)
+
+
+def halves(ref):
+    def store(g, value):
+        lanes = value.shape[1] // 2
         for c in range(2):
-            s_buf[c, at + g] = value[:, c * lanes : (c + 1) * lanes]
-
-    groups = e_buf.shape[2] // 8
-    apply_gate(parts_of(e_buf), store_s, weights.at[1], bonds.at[1], groups, groups)
-
-
-def own_kernel(order_ref, bits_ref, own_ref, gates_ref, bonds_ref, out_ref, *refs):
-    q_buf, e_buf, s_buf, gate_buf, bond_buf, gate_rows_buf, weights, g_sem, i_sem, o_sem = refs
-    copy = pltpu.make_async_copy(own_ref, q_buf, i_sem)
-    copy.start()
-    wait_all(fetch(order_ref, bits_ref, 4, gates_ref, bonds_ref, gate_buf, bond_buf, g_sem))
-    tiles = list(range(e_buf.shape[1]))
-    for k in range(2):
-        make_weight(gate_buf.at[k], gate_rows_buf, weights.at[k], tiles)
-    copy.wait()
-    fifth_sixth(q_buf, e_buf, s_buf, 0, weights, bond_buf)
-    copy = pltpu.make_async_copy(s_buf, out_ref, o_sem)
-    copy.start()
-    copy.wait()
-
-
-def tail_kernel(order_ref, bits_ref, done_ref, got_ref, gates_ref, bonds_ref, out_ref, *refs):
-    q_buf, e_buf, s_buf, f_buf, y_buf, gate_buf, bond_buf, gate_rows_buf, weights, g_sem, i_sem, y_sem = refs
-    core = lax.axis_index("inner")
-    half = s_buf.shape[1] // 2
-    got = pltpu.make_async_copy(got_ref, q_buf, i_sem.at[0])
-    got.start()
-    done = pltpu.make_async_copy(done_ref, s_buf.at[:, pl.ds(core * half, half)], i_sem.at[1])
-    done.start()
-    wait_all(fetch(order_ref, bits_ref, 4, gates_ref, bonds_ref, gate_buf, bond_buf, g_sem))
-    tiles = list(range(e_buf.shape[1]))
-    for k in range(4):
-        make_weight(gate_buf.at[k], gate_rows_buf, weights.at[k], tiles if k < 2 else None)
-    got.wait()
-    fifth_sixth(q_buf, e_buf, s_buf, (1 - core) * half, weights, bond_buf)
-    done.wait()
-    lanes = f_buf.shape[-1]
-    groups = f_buf.shape[1]
+            ref[c, g] = value[:, c * lanes : (c + 1) * lanes]
+
+    return store
+
+
+def stacked(refs, c):
+    def load(g):
+        values = [ref[(*lead, slice(None), pl.ds(g * 8, 8), slice(None))] for ref, lead in refs(c)]
+        value = jnp.concatenate(values, axis=0)
+        return value.reshape(-1, value.shape[-1])
+
+    return load
+
+
+def pair_of(refs):
+    loads = [stacked(refs, c) for c in range(2)]
+    return lambda g: [load(g) for load in loads]
+
+
+def join_kernel(weights, bonds, *refs, n, chunk):
+    near, far, (own, other) = refs[: n // 2], refs[n // 2 : n], refs[n:]
+    groups = own.shape[0]
+    load = stacked(lambda c: [(r, (chunk,)) for r in near] + [(r, ()) for r in far], 0)
 
     def store(g, value):
-        for c in range(2):
-            f_buf[c, g] = value[:, c * lanes : (c + 1) * lanes]
-
-    apply_gate(parts_of(s_buf), store, weights.at[2], bond_buf.at[2], groups, 8)
+        lanes = own.shape[-1]
+        own[g] = value[:, :lanes]
+        other[g] = value[:, lanes:]
+
+    apply_gate(lambda g: [load(g)], store, weights.at[0], bonds.at[0], groups)
+
+
+def fifth(q, e, weights, bonds):
+    load = tiles_of(q)
+    apply_gate(lambda g: [load(g)], halves(e), weights.at[1], bonds.at[1], q.shape[1] // 8)
+
+
+def sixth(e0, e1, s, weights, bonds):
+    load = pair_of(lambda c: [(e0, (c,)), (e1, (c,))])
+    apply_gate(load, halves(s), weights.at[2], bonds.at[2], s.shape[1])
+
+
+def fifth_kernel(weights, bonds, q, e):
+    fifth(q, e, weights, bonds)
+
+
+def own_kernel(weights, bonds, e0, q1, s, e1):
+    fifth(q1, e1, weights, bonds)
+    sixth(e0, e1, s, weights, bonds)
+
+
+def tail_kernel(weights, bonds, s_own, e0, q1, out_ref, e1, s_got, f, y, y_sem):
+    fifth(q1, e1, weights, bonds)
+    sixth(e0, e1, s_got, weights, bonds)
+    groups = f.shape[1]
+    lanes = f.shape[-1]
+    apply_gate(pair_of(lambda c: [(s_own, (c,)), (s_got, (c,))]), halves(f), weights.at[3], bonds.at[3], groups)
 
     def y_copy(g, c):
         return pltpu.make_async_copy(
-            y_buf.at[c, g], out_ref.at[pl.ds(pl.multiple_of(g * lanes, lanes), lanes), c, :], y_sem.at[c, g]
+            y.at[c, g], out_ref.at[pl.ds(g * lanes, lanes), c, :], y_sem.at[c, g]
         )
 
-    def store_y(g, value):
-        for c in range(2):
-            y_buf[c, g] = value[:, c * lanes : (c + 1) * lanes]
-            y_copy(g, c).start()
-
-    apply_gate(parts_of(f_buf), store_y, weights.at[3], bond_buf.at[3], groups, 8)
-    for g in range(groups):
-        for c in range(2):
-            y_copy(g, c).wait()
+    def leave(some):
+        start_all([y_copy(g, c) for g in some for c in range(2)])
+
+    apply_gate(
+        parts_of(f), halves(y), weights.at[4], bonds.at[4], groups, after=leave, batch=groups // TAIL_BATCHES
+    )
+    wait_all([y_copy(g, c) for g in range(groups) for c in range(2)])
+
+
+def inside(body, ins, outs, scratch=(), work=4, out_specs=None):
+    here = pl.BlockSpec(memory_space=pltpu.VMEM)
+    dim = ins[0].shape[-1] // 2
+    return pl.pallas_call(
+        body,
+        out_shape=[jax.ShapeDtypeStruct(shape, jnp.float32) for shape in outs],
+        in_specs=[here] * len(ins),
+        out_specs=out_specs or [here] * len(outs),
+        scratch_shapes=list(scratch),
+        compiler_params=pltpu.CompilerParams(vmem_limit_bytes=VMEM_LIMIT),
+        cost_estimate=pl.CostEstimate(flops=work * 4 * dim**4, bytes_accessed=0, transcendentals=0),
+    )(*ins)
 
 
 def launch(body, scalars, ins, out_shape, scratch, steps, dim, work, limit=VMEM_LIMIT):
@@ -524,6 +534,33 @@
     )(*scalars, *ins)
 
 
+def prepare(scalars, gates, bonds, n):
+    dim = gates.shape[-1]
+    anywhere = pl.BlockSpec(memory_space=pl.ANY)
+    here = pl.BlockSpec(memory_space=pltpu.VMEM)
+    return pl.pallas_call(
+        functools.partial(prep_kernel, n=n),
+        out_shape=[
+            jax.ShapeDtypeStruct((5, 2 * dim, 2 * dim), jnp.bfloat16),
+            jax.ShapeDtypeStruct((5, 2, dim), jnp.float32),
+        ],
+        grid_spec=pltpu.PrefetchScalarGridSpec(
+            num_scalar_prefetch=2,
+            grid=(),
+            in_specs=[anywhere] * 2,
+            out_specs=[here] * 2,
+            scratch_shapes=[
+                pltpu.VMEM((5, 2, dim, dim), jnp.bfloat16),
+                pltpu.VMEM((5, 2, dim), jnp.float32),
+                pltpu.VMEM((2, dim, dim), jnp.float32),
+                pltpu.SemaphoreType.DMA((5, 2)),
+            ],
+        ),
+        compiler_params=pltpu.CompilerParams(vmem_limit_bytes=VMEM_LIMIT),
+        cost_estimate=pl.CostEstimate(flops=4 * dim**4, bytes_accessed=0, transcendentals=0),
+    )(*scalars, gates, bonds)
+
+
 def swap(piece, axis, k):
     n = lax.axis_size(axis)
     return lax.ppermute(piece, axis, [(i, i ^ k) for i in range(n)])
@@ -544,17 +581,17 @@
         functools.partial(head_kernel, n=n),
         scalars,
         (x, gates, bonds),
-        [piece] * half + [(rows, dim)],
-        ([(2, m, dim, dim), (rows, dim), (rows, dim)] + mids, [(2, m), (half,), ()]),
+        [piece[1:]] * n + [(rows, dim)],
+        ([(2, m, dim, dim), (rows, dim), (rows, dim)] + mids, [(2, m), (half, 2), ()]),
         3,
         dim,
         8,
         None,
     )
     sent = []
-    for k in range(half):
-        sent.append(swap(far[k], "outer", half + k))
-    far = sent
+    for chunk in range(2):
+        for k in range(half):
+            sent.append(swap(far[2 * k + chunk], "outer", half + k))
     near = launch(
         functools.partial(near_kernel, n=n),
         scalars,
@@ -566,29 +603,36 @@
         4,
     )
     near = [near[0]] + [swap(near[k], "outer", k) for k in range(1, half)]
-    own, other = launch(
-        functools.partial(join_kernel, n=n),
-        scalars,
-        (gates, bonds, *near, *far),
-        [block, block],
-        ([(2, m, dim, dim), block, block], [(n,), (2, 2)]),
-        1,
-        dim,
-        4,
-    )
-    got = swap(other, "inner", 1)
-    done = launch(
-        own_kernel, scalars, (own, gates, bonds), [mids[1]], ([block, block, mids[1]], [(), ()]), 2, dim, 4
-    )[0]
-    out = launch(
+    prepared = prepare(scalars, gates, bonds, n)
+    q = (m, dim // 2, dim)
+    e = (2, m // 2, dim // 2, dim)
+    e_buf = pltpu.VMEM(e, jnp.float32)
+    s = mids[1]
+    joined = []
+    for chunk in range(2):
+        joined.append(
+            inside(
+                functools.partial(join_kernel, n=n, chunk=chunk),
+                [*prepared, *near, *sent[chunk * half : (chunk + 1) * half]],
+                [q, q],
+                work=2,
+            )
+        )
+    own, other = zip(*joined)
+    got = []
+    for chunk in range(2):
+        got.append(swap(other[chunk], "inner", 1))
+    e_own = inside(fifth_kernel, [*prepared, own[0]], [e], work=1)[0]
+    e_got = inside(fifth_kernel, [*prepared, got[0]], [e], work=1)[0]
+    s_own = inside(own_kernel, [*prepared, e_own, own[1]], [s], [e_buf], work=3)[0]
+    full = pltpu.VMEM((2, m, dim, dim), jnp.float32)
+    out = inside(
         tail_kernel,
-        scalars,
-        (done, got, gates, bonds),
+        [*prepared, s_own, e_got, got[1]],
         [(rows, 2, dim)],
-        ([block, block, (2, m, dim, dim), (2, m, dim, dim), (2, m, dim, dim)], [(2,), (2, m)]),
-        4,
-        dim,
-        12,
+        [e_buf, pltpu.VMEM(s, jnp.float32), full, full, pltpu.SemaphoreType.DMA((2, m))],
+        work=12,
+        out_specs=[pl.BlockSpec(memory_space=pl.ANY)],
     )[0]
     return out.transpose(1, 0, 2).reshape(2, rows * dim)
 

time: 75.8 us -> 64.4 us (0.85)
  the two profiles are of different devices: /device:TPU:19 before, /device:TPU:13 now
where the time goes in v2:
time: 64.4 us; the launch traced here: 63.2 us
  starting transfers between devices  23.4 us (36%)
  waiting for transfers between devices  21.7 us (34%)
  Pallas kernels  16.7 us (26%)
  local copies, waits for them, and re-layouts  1.26 us (2%)
    ppermute x13, starting transfers between devices, swap(): return lax.ppermute(piece, axis, [(i, i ^ k) for i in range(n)])  23.4 us
    ppermute x13, waiting for transfers between devices, swap(): return lax.ppermute(piece, axis, [(i, i ^ k) for i in range(n)])  21.7 us
    pallas_call x2, Pallas kernels, launch(): pl.pallas_call(body, out_shape=[jax.ShapeDtypeStruct(shape, jnp.float32)...  8.61 us
    pallas_call x6, Pallas kernels, inside(): pl.pallas_call(body, out_shape=[jax.ShapeDtypeStruct(shape, jnp.float32)...  6.42 us
    pallas_call x1, Pallas kernels, prepare(): pl.pallas_call(functools.partial(prep_kernel, n=n), out_shape=[jax.ShapeD...  1.69 us
  transfers between devices with their start and end apart: 13, of which 7 were waited for; matrix products, arithmetic and copies ran while one was open for 0% of the time, Pallas kernels for 11%

profile of v2, /device:TPU:13, one launch (start us, length us, event | category | flops | bytes accessed | tf_op | source)
XLA Modules:
  0.0 63.2 jit_solution(3283244318571365724)
XLA Ops:
  0.0 6.3 %shard_map.56 = (f32[2,128,128]{2,1,0:T(8,128)}, f32[2,128,128]{2,1,0:T(8,128)}, f32[2,128,128]{2,1,0:T(8,128)}, f32[2,128,128]{2,1,0:T(8,128)}, f32[2,128,128]{...) custom-call(s32[8]{0:T(128)} %order_ref.5, ...), custom_call_target="tpu_custom_call" | custom-call | flops 8589934592 | tf_op jit(solution)/shard_map/pallas_call | solution.py:520
  6.4 2.4 %collective-permute-start.3 = (f32[2,128,128]{2,1,0:T(8,128)}, f32[2,128,128]{2,1,0:T(8,128)S(1)}, u32[]{:S(2)}, u32[]{:S(2)}) collective-permute-start(f32[2,128,128]{2,1,0:T(8,128)} %get-tuple-element.31), channel_id=1, source_target_pairs={{0,8},{2,10},{4,12},{6,14},{8,0},{10,2},{12,4},{14,6},{1,9},{3,11}... | collective-permute-start | bytes 393224 | tf_op jit(solution)/shard_map/ppermute | solution.py:566
  8.8 1.2 %copy-done.4 = f32[2048,128]{1,0:T(8,128)S(1)} copy-done((f32[2048,128]{1,0:T(8,128)S(1)}, f32[2048,128]{1,0:T(8,128)}, u32[]{:S(2)}) %copy-start.4) | copy-done | bytes 1048600
  10.0 2.3 %shard_map.57 = (f32[2,2,128,128]{3,2,1,0:T(8,128)S(1)}, f32[2,2,128,128]{3,2,1,0:T(8,128)S(1)}, f32[2,2,128,128]{3,2,1,0:T(8,128)S(1)}, f32[2,2,128,128]{3,2,1,0:T(8,128)S(1)}) custom-call(s32[8]{0:T(128)S(1)} %copy-done.2, s32[8]{0:T(128)S(1)} %copy-done.3, f32[2048,128]{1,0:T(8,128)S(1)} %copy-done.4, bf16[8,2,128,128]{3,2,1,0:T(8,128)(2,1)S(1)} %copy-done, ...), custom_call_target="tpu_custom_call" | custom-call | flops 4294967296 | tf_op jit(solution)/shard_map/pallas_call | solution.py:520
  12.3 1.3 %collective-permute-start = (f32[2,2,128,128]{3,2,1,0:T(8,128)S(1)}, f32[2,2,128,128]{3,2,1,0:T(8,128)S(1)}, u32[]{:S(2)}, u32[]{:S(2)}) collective-permute-start(f32[2,2,128,128]{3,2,1,0:T(8,128)S(1)} %get-tuple-element.28), channel_id=1, source_target_pairs={{0,2},{2,0},{4,6},{6,4},{8,10},{10,8},{12,14},{14,12},{1,3},{3,1},... | collective-permute-start | bytes 786440 | tf_op jit(solution)/shard_map/ppermute | solution.py:566
  13.8 1.2 %collective-permute-start.2 = (f32[2,2,128,128]{3,2,1,0:T(8,128)S(1)}, f32[2,2,128,128]{3,2,1,0:T(8,128)S(1)}, u32[]{:S(2)}, u32[]{:S(2)}) collective-permute-start(f32[2,2,128,128]{3,2,1,0:T(8,128)S(1)} %get-tuple-element.30), channel_id=1, source_target_pairs={{0,6},{2,4},{4,2},{6,0},{8,14},{10,12},{12,10},{14,8},{1,7},{3,5},... | collective-permute-start | bytes 786440 | tf_op jit(solution)/shard_map/ppermute | solution.py:566
  15.0 2.8 %collective-permute-done.3.refs_4_ = f32[2,128,128]{2,1,0:T(8,128)S(1)} collective-permute-done((f32[2,128,128]{2,1,0:T(8,128)}, f32[2,128,128]{2,1,0:T(8,128)S(1)}, u32[]{:S(2)}, u32[]{:S(2)}) %collective-permute-start.3) | collective-permute-done | bytes 131104 | tf_op jit(solution)/shard_map/ppermute | solution.py:566
  17.8 2.9 %collective-permute-done.4.refs_5_ = f32[2,128,128]{2,1,0:T(8,128)S(1)} collective-permute-done((f32[2,128,128]{2,1,0:T(8,128)}, f32[2,128,128]{2,1,0:T(8,128)S(1)}, u32[]{:S(2)}, u32[]{:S(2)}) %collective-permute-start.4) | collective-permute-done | bytes 131104 | tf_op jit(solution)/shard_map/ppermute | solution.py:566
  20.7 1.7 %shard_map.55 = (bf16[5,256,256]{2,1,0:T(8,128)(2,1)S(1)}, f32[5,2,128]{2,1,0:T(2,128)S(1)}) custom-call(s32[8]{0:T(128)S(1)} %copy-done.2, s32[8]{0:T(128)S(1)} %copy-done.3, bf16[8,2,128,128]{3,2,1,0:T(8,128)(2,1)S(1)} %copy-done, f32[8,2,2,128]{3,2,1,0:T(2,128)S(1)} %copy-done.1), custom_call_target="tpu_custom_call" | custom-call | flops 1073741824 | tf_op jit(solution)/shard_map/pallas_call | solution.py:541
  22.4 1.0 %collective-permute-done.5.refs_6_ = f32[2,128,128]{2,1,0:T(8,128)S(1)} collective-permute-done((f32[2,128,128]{2,1,0:T(8,128)S(1)}, f32[2,128,128]{2,1,0:T(8,128)S(1)}, u32[]{:S(2)}, u32[]{:S(2)}) %collective-permute-start.5) | collective-permute-done | bytes 131104 | tf_op jit(solution)/shard_map/ppermute | solution.py:566
  23.4 7.8 %collective-permute-start.7 = (f32[2,128,128]{2,1,0:T(8,128)S(1)}, f32[2,128,128]{2,1,0:T(8,128)S(1)}, u32[]{:S(2)}, u32[]{:S(2)}) collective-permute-start(f32[2,128,128]{2,1,0:T(8,128)S(1)} %copy-done.8), channel_id=1, source_target_pairs={{0,8},{2,10},{4,12},{6,14},{8,0},{10,2},{12,4},{14,6},{1,9},{3,11}... | collective-permute-start | bytes 393224 | tf_op jit(solution)/shard_map/ppermute | solution.py:566
  31.2 3.8 %collective-permute-start.8 = (f32[2,128,128]{2,1,0:T(8,128)S(1)}, f32[2,128,128]{2,1,0:T(8,128)S(1)}, u32[]{:S(2)}, u32[]{:S(2)}) collective-permute-start(f32[2,128,128]{2,1,0:T(8,128)S(1)} %copy-done.7), channel_id=1, source_target_pairs={{0,10},{2,8},{4,14},{6,12},{8,2},{10,0},{12,6},{14,4},{1,11},{3,9}... | collective-permute-start | bytes 393224 | tf_op jit(solution)/shard_map/ppermute | solution.py:566
  35.7 0.5 shard_map.58
  36.2 5.0 %collective-permute-start.11 = (f32[16,64,128]{2,1,0:T(8,128)S(1)}, f32[16,64,128]{2,1,0:T(8,128)S(1)}, u32[]{:S(2)}, u32[]{:S(2)}) collective-permute-start(f32[16,64,128]{2,1,0:T(8,128)S(1)} %get-tuple-element.41), channel_id=1, source_target_pairs={{0,1},{1,0},{2,3},{3,2},{4,5},{5,4},{6,7},{7,6},{8,9},{9,8},{10,11... | collective-permute-start | bytes 1572872 | tf_op jit(solution)/shard_map/ppermute | solution.py:566
  41.3 5.9 %collective-permute-done.7.refs_4_ = f32[2,128,128]{2,1,0:T(8,128)S(1)} collective-permute-done((f32[2,128,128]{2,1,0:T(8,128)S(1)}, f32[2,128,128]{2,1,0:T(8,128)S(1)}, u32[]{:S(2)}, u32[]{:S(2)}) %collective-permute-start.7) | collective-permute-done | bytes 131104 | tf_op jit(solution)/shard_map/ppermute | solution.py:566
  47.1 2.8 %collective-permute-done.8.refs_5_ = f32[2,128,128]{2,1,0:T(8,128)S(1)} collective-permute-done((f32[2,128,128]{2,1,0:T(8,128)S(1)}, f32[2,128,128]{2,1,0:T(8,128)S(1)}, u32[]{:S(2)}, u32[]{:S(2)}) %collective-permute-start.8) | collective-permute-done | bytes 131104 | tf_op jit(solution)/shard_map/ppermute | solution.py:566
  49.9 4.0 %collective-permute-done.9.refs_6_ = f32[2,128,128]{2,1,0:T(8,128)S(1)} collective-permute-done((f32[2,128,128]{2,1,0:T(8,128)S(1)}, f32[2,128,128]{2,1,0:T(8,128)S(1)}, u32[]{:S(2)}, u32[]{:S(2)}) %collective-permute-start.9) | collective-permute-done | bytes 131104 | tf_op jit(solution)/shard_map/ppermute | solution.py:566
  53.9 2.4 %collective-permute-done.10.refs_7_ = f32[2,128,128]{2,1,0:T(8,128)S(1)} collective-permute-done((f32[2,128,128]{2,1,0:T(8,128)S(1)}, f32[2,128,128]{2,1,0:T(8,128)S(1)}, u32[]{:S(2)}, u32[]{:S(2)}) %collective-permute-start.10) | collective-permute-done | bytes 131104 | tf_op jit(solution)/shard_map/ppermute | solution.py:566
  56.4 0.5 shard_map.60
  56.9 0.9 %collective-permute-start.12 = (f32[16,64,128]{2,1,0:T(8,128)S(1)}, f32[16,64,128]{2,1,0:T(8,128)S(1)}, u32[]{:S(2)}, u32[]{:S(2)}) collective-permute-start(f32[16,64,128]{2,1,0:T(8,128)S(1)} %get-tuple-element.42), channel_id=1, source_target_pairs={{0,1},{1,0},{2,3},{3,2},{4,5},{5,4},{6,7},{7,6},{8,9},{9,8},{10,11... | collective-permute-start | bytes 1572872 | tf_op jit(solution)/shard_map/ppermute | solution.py:566
  57.8 0.4 shard_map.59.e0
  58.2 0.9 %shard_map.61.s_own = f32[2,8,128,128]{3,2,1,0:T(8,128)S(1)} custom-call(bf16[5,256,256]{2,1,0:T(8,128)(2,1)S(1)} %get-tuple-element.24.weights, f32[5,2,128]{2,1,0:T(2,128)S(1)} %get-tuple-element.25.bonds, f32[2,8,64,128]{3,2,1,0:T(8,128)S(1)} %shard_map.59.e0, f32[16,64,128]{2,1,0:T(8,128)S(1)} %get-tuple-element.40.q1), custom_call_target="tpu_custom_call" | custom-call | flops 3221225472 | tf_op jit(solution)/shard_map/pallas_call | solution.py:499
  59.1 0.4 shard_map.62.e0
  59.5 3.7 %shard_map.63 = f32[2048,2,128]{2,1,0:T(2,128)} custom-call(bf16[5,256,256]{2,1,0:T(8,128)(2,1)S(1)} %get-tuple-element.24.weights, f32[5,2,128]{2,1,0:T(2,128)S(1)} %get-tuple-element.25.bonds, f32[2,8,128,128]{3,2,1,0:T(8,128)S(1)} %shard_map.61.s_own, f32[2,8,64,128]{3,2,1,0:T(8,128)S(1)} %shard_map.62.e0, f32[16,64,128]{2,1,0:T(8,128)S(1)} %collective-permute-done.12.q1), custom_call_target="tpu_custom_call" | custom-call | flops 12884901888 | tf_op jit(solution)/shard_map/pallas_call | solution.py:499
  (33 shorter events, 1.0 us)
Async XLA Ops:
  0.0 8.8 %copy-start = (bf16[8,2,128,128]{3,2,1,0:T(8,128)(2,1)S(1)}, bf16[8,2,128,128]{3,2,1,0:T(8,128)(2,1)}, u32[]{:S(2)}) copy-start(bf16[8,2,128,128]{3,2,1,0:T(8,128)(2,1)} %gates_ref.5) | copy-start | bytes 1572868
  0.0 8.8 %copy-start.1 = (f32[8,2,2,128]{3,2,1,0:T(2,128)S(1)}, f32[8,2,2,128]{3,2,1,0:T(2,128)}, u32[]{:S(2)}) copy-start(f32[8,2,2,128]{3,2,1,0:T(2,128)} %bonds_ref.5) | copy-start | bytes 49156
  0.0 8.8 %copy-start.2 = (s32[8]{0:T(128)S(1)}, s32[8]{0:T(128)}, u32[]{:S(2)}) copy-start(s32[8]{0:T(128)} %order_ref.5) | copy-start | bytes 100
  0.0 8.8 %copy-start.3 = (s32[8]{0:T(128)S(1)}, s32[8]{0:T(128)}, u32[]{:S(2)}) copy-start(s32[8]{0:T(128)} %bits_ref.5) | copy-start | bytes 100
  6.4 11.4 %collective-permute-start.3 = (f32[2,128,128]{2,1,0:T(8,128)}, f32[2,128,128]{2,1,0:T(8,128)S(1)}, u32[]{:S(2)}, u32[]{:S(2)}) collective-permute-start(f32[2,128,128]{2,1,0:T(8,128)} %get-tuple-element.31), channel_id=1, source_target_pairs={{0,8},{2,10},{4,12},{6,14},{8,0},{10,2},{12,4},{14,6},{1,9},{3,11}... | collective-permute-start | bytes 393224 | tf_op jit(solution)/shard_map/ppermute | solution.py:566
  8.7 11.9 %collective-permute-start.4 = (f32[2,128,128]{2,1,0:T(8,128)}, f32[2,128,128]{2,1,0:T(8,128)S(1)}, u32[]{:S(2)}, u32[]{:S(2)}) collective-permute-start(f32[2,128,128]{2,1,0:T(8,128)} %get-tuple-element.32), channel_id=1, source_target_pairs={{0,10},{2,8},{4,14},{6,12},{8,2},{10,0},{12,6},{14,4},{1,11},{3,9}... | collective-permute-start | bytes 393224 | tf_op jit(solution)/shard_map/ppermute | solution.py:566
  8.8 1.2 %copy-start.4 = (f32[2048,128]{1,0:T(8,128)S(1)}, f32[2048,128]{1,0:T(8,128)}, u32[]{:S(2)}) copy-start(f32[2048,128]{1,0:T(8,128)} %get-tuple-element.26.near_ref) | copy-start | bytes 3145732
  10.0 7.8 %copy-start.10 = (f32[2,128,128]{2,1,0:T(8,128)S(1)}, f32[2,128,128]{2,1,0:T(8,128)}, u32[]{:S(2)}) copy-start(f32[2,128,128]{2,1,0:T(8,128)} %get-tuple-element.33) | copy-start | bytes 393220
  10.0 10.7 %copy-start.9 = (f32[2,128,128]{2,1,0:T(8,128)S(1)}, f32[2,128,128]{2,1,0:T(8,128)}, u32[]{:S(2)}) copy-start(f32[2,128,128]{2,1,0:T(8,128)} %get-tuple-element.34) | copy-start | bytes 393220
  12.3 11.1 %copy-start.8 = (f32[2,128,128]{2,1,0:T(8,128)S(1)}, f32[2,128,128]{2,1,0:T(8,128)}, u32[]{:S(2)}) copy-start(f32[2,128,128]{2,1,0:T(8,128)} %get-tuple-element.36) | copy-start | bytes 393220
  12.3 18.9 %copy-start.7 = (f32[2,128,128]{2,1,0:T(8,128)S(1)}, f32[2,128,128]{2,1,0:T(8,128)}, u32[]{:S(2)}) copy-start(f32[2,128,128]{2,1,0:T(8,128)} %get-tuple-element.37) | copy-start | bytes 393220
  12.3 22.7 %copy-start.6 = (f32[2,128,128]{2,1,0:T(8,128)S(1)}, f32[2,128,128]{2,1,0:T(8,128)}, u32[]{:S(2)}) copy-start(f32[2,128,128]{2,1,0:T(8,128)} %get-tuple-element.38) | copy-start | bytes 393220
  12.3 23.1 %copy-start.5 = (f32[2,128,128]{2,1,0:T(8,128)S(1)}, f32[2,128,128]{2,1,0:T(8,128)}, u32[]{:S(2)}) copy-start(f32[2,128,128]{2,1,0:T(8,128)} %get-tuple-element.39) | copy-start | bytes 393220
  12.3 22.7 %collective-permute-start = (f32[2,2,128,128]{3,2,1,0:T(8,128)S(1)}, f32[2,2,128,128]{3,2,1,0:T(8,128)S(1)}, u32[]{:S(2)}, u32[]{:S(2)}) collective-permute-start(f32[2,2,128,128]{3,2,1,0:T(8,128)S(1)} %get-tuple-element.28), channel_id=1, source_target_pairs={{0,2},{2,0},{4,6},{6,4},{8,10},{10,8},{12,14},{14,12},{1,3},{3,1},... | collective-permute-start | bytes 786440 | tf_op jit(solution)/shard_map/ppermute | solution.py:566
  13.6 21.7 %collective-permute-start.1 = (f32[2,2,128,128]{3,2,1,0:T(8,128)S(1)}, f32[2,2,128,128]{3,2,1,0:T(8,128)S(1)}, u32[]{:S(2)}, u32[]{:S(2)}) collective-permute-start(f32[2,2,128,128]{3,2,1,0:T(8,128)S(1)} %get-tuple-element.29), channel_id=1, source_target_pairs={{0,4},{2,6},{4,0},{6,2},{8,12},{10,14},{12,8},{14,10},{1,5},{3,7},... | collective-permute-start | bytes 786440 | tf_op jit(solution)/shard_map/ppermute | solution.py:566
  13.8 21.9 %collective-permute-start.2 = (f32[2,2,128,128]{3,2,1,0:T(8,128)S(1)}, f32[2,2,128,128]{3,2,1,0:T(8,128)S(1)}, u32[]{:S(2)}, u32[]{:S(2)}) collective-permute-start(f32[2,2,128,128]{3,2,1,0:T(8,128)S(1)} %get-tuple-element.30), channel_id=1, source_target_pairs={{0,6},{2,4},{4,2},{6,0},{8,14},{10,12},{12,10},{14,8},{1,7},{3,5},... | collective-permute-start | bytes 786440 | tf_op jit(solution)/shard_map/ppermute | solution.py:566
  17.8 5.6 %collective-permute-start.5 = (f32[2,128,128]{2,1,0:T(8,128)S(1)}, f32[2,128,128]{2,1,0:T(8,128)S(1)}, u32[]{:S(2)}, u32[]{:S(2)}) collective-permute-start(f32[2,128,128]{2,1,0:T(8,128)S(1)} %copy-done.10), channel_id=1, source_target_pairs={{0,12},{2,14},{4,8},{6,10},{8,4},{10,6},{12,0},{14,2},{1,13},{3,15... | collective-permute-start | bytes 393224 | tf_op jit(solution)/shard_map/ppermute | solution.py:566
  20.7 10.5 %collective-permute-start.6 = (f32[2,128,128]{2,1,0:T(8,128)S(1)}, f32[2,128,128]{2,1,0:T(8,128)S(1)}, u32[]{:S(2)}, u32[]{:S(2)}) collective-permute-start(f32[2,128,128]{2,1,0:T(8,128)S(1)} %copy-done.9), channel_id=1, source_target_pairs={{0,14},{2,12},{4,10},{6,8},{8,6},{10,4},{12,2},{14,0},{1,15},{3,13... | collective-permute-start | bytes 393224 | tf_op jit(solution)/shard_map/ppermute | solution.py:566
  23.4 23.8 %collective-permute-start.7 = (f32[2,128,128]{2,1,0:T(8,128)S(1)}, f32[2,128,128]{2,1,0:T(8,128)S(1)}, u32[]{:S(2)}, u32[]{:S(2)}) collective-permute-start(f32[2,128,128]{2,1,0:T(8,128)S(1)} %copy-done.8), channel_id=1, source_target_pairs={{0,8},{2,10},{4,12},{6,14},{8,0},{10,2},{12,4},{14,6},{1,9},{3,11}... | collective-permute-start | bytes 393224 | tf_op jit(solution)/shard_map/ppermute | solution.py:566
  31.2 18.8 %collective-permute-start.8 = (f32[2,128,128]{2,1,0:T(8,128)S(1)}, f32[2,128,128]{2,1,0:T(8,128)S(1)}, u32[]{:S(2)}, u32[]{:S(2)}) collective-permute-start(f32[2,128,128]{2,1,0:T(8,128)S(1)} %copy-done.7), channel_id=1, source_target_pairs={{0,10},{2,8},{4,14},{6,12},{8,2},{10,0},{12,6},{14,4},{1,11},{3,9}... | collective-permute-start | bytes 393224 | tf_op jit(solution)/shard_map/ppermute | solution.py:566
  35.0 18.9 %collective-permute-start.9 = (f32[2,128,128]{2,1,0:T(8,128)S(1)}, f32[2,128,128]{2,1,0:T(8,128)S(1)}, u32[]{:S(2)}, u32[]{:S(2)}) collective-permute-start(f32[2,128,128]{2,1,0:T(8,128)S(1)} %copy-done.6), channel_id=1, source_target_pairs={{0,12},{2,14},{4,8},{6,10},{8,4},{10,6},{12,0},{14,2},{1,13},{3,15... | collective-permute-start | bytes 393224 | tf_op jit(solution)/shard_map/ppermute | solution.py:566
  35.4 21.0 %collective-permute-start.10 = (f32[2,128,128]{2,1,0:T(8,128)S(1)}, f32[2,128,128]{2,1,0:T(8,128)S(1)}, u32[]{:S(2)}, u32[]{:S(2)}) collective-permute-start(f32[2,128,128]{2,1,0:T(8,128)S(1)} %copy-done.5), channel_id=1, source_target_pairs={{0,14},{2,12},{4,10},{6,8},{8,6},{10,4},{12,2},{14,0},{1,15},{3,13... | collective-permute-start | bytes 393224 | tf_op jit(solution)/shard_map/ppermute | solution.py:566
  36.2 22.9 %collective-permute-start.11 = (f32[16,64,128]{2,1,0:T(8,128)S(1)}, f32[16,64,128]{2,1,0:T(8,128)S(1)}, u32[]{:S(2)}, u32[]{:S(2)}) collective-permute-start(f32[16,64,128]{2,1,0:T(8,128)S(1)} %get-tuple-element.41), channel_id=1, source_target_pairs={{0,1},{1,0},{2,3},{3,2},{4,5},{5,4},{6,7},{7,6},{8,9},{9,8},{10,11... | collective-permute-start | bytes 1572872 | tf_op jit(solution)/shard_map/ppermute | solution.py:566
  56.9 2.6 %collective-permute-start.12 = (f32[16,64,128]{2,1,0:T(8,128)S(1)}, f32[16,64,128]{2,1,0:T(8,128)S(1)}, u32[]{:S(2)}, u32[]{:S(2)}) collective-permute-start(f32[16,64,128]{2,1,0:T(8,128)S(1)} %get-tuple-element.42), channel_id=1, source_target_pairs={{0,1},{1,0},{2,3},{3,2},{4,5},{5,4},{6,7},{7,6},{8,9},{9,8},{10,11... | collective-permute-start | bytes 1572872 | tf_op jit(solution)/shard_map/ppermute | solution.py:566
